TPU v7x, 32 devices: a whole 2x2x4 slice. The times are simulated.
32 devices in a mesh: dp: 16 (over z, x, core), tensor: 2 (over y).
Axes of the slice: x: 2, y: 2, z: 4, core: 2. Of those that a mesh axis runs over, the one named last changes fastest.
Arguments:
- tokens: bfloat16 [2048, 512], P('dp'), may hold values from -10 to 10
- lengths: int32 [16], P('dp'), may hold values from 32 to 128, as said below
- cotangent: float32 [2048, 512], P('dp'), may hold values from -6 to 6
- params: float32 [1, 2, 3157504], P(None, 'tensor', 'dp'), may hold values from -2 to 2
- shared: float32 [1, 7168], P(None, 'dp'), may hold values from -0.6 to 0.6
- first_moment: float32 [1, 2, 3157504], P(None, 'tensor', 'dp'), may hold values from -4 to 4
- second_moment: float32 [1, 2, 3157504], P(None, 'tensor', 'dp'), may hold values from 0.01 to 1
- first_shared: float32 [1, 7168], P(None, 'dp'), may hold values from -4 to 4
- second_shared: float32 [1, 7168], P(None, 'dp'), may hold values from 4.096 to 40.96
Outputs:
- result: float32 [2048, 512], P('dp')
- grad_tokens: float32 [2048, 512], P('dp')
- grad_params: float32 [1, 2, 3157504], P(None, 'tensor', 'dp')
- grad_shared: float32 [1, 7168], P(None, 'dp')
- new_params: float32 [1, 2, 3157504], P(None, 'tensor', 'dp')
- new_shared: float32 [1, 7168], P(None, 'dp')
- new_first_moment: float32 [1, 2, 3157504], P(None, 'tensor', 'dp')
- new_second_moment: float32 [1, 2, 3157504], P(None, 'tensor', 'dp')
- new_first_shared: float32 [1, 7168], P(None, 'dp')
- new_second_shared: float32 [1, 7168], P(None, 'dp')
Inputs may be any that keep to these rules, and one draw needn't show every extreme that they name: Valid tokens lead each sequence. The first sequence holds 32 valid tokens and the last 128; lengths grow with the sequence index, with a jitter.
All inputs are finite; a program needn't handle non-finite values.
Results may differ from a plain program's by a relative error of at most 0.02.
Values may be sent and summed in bfloat16 or wider, within the bound.
No kernel may reach another device: no remote copies, remote signals or barrier semaphores. Data moves between devices by JAX's collectives and lax.ppermute only.
A program may use at most 128 MiB of HBM per device.

v0:
```python
from functools import partial
import math

import jax
import jax.numpy as jnp
from jax import lax
from jax.experimental import pallas as pl
from jax.experimental.pallas import tpu as pltpu
from jax.sharding import PartitionSpec as P


D = 512
FF = 2048
HEADS = 8
HEAD_DIM = 64
KERNEL = 31
SEQ_LEN = 128


NORM_EPS = 1e-05
BATCH_EPS = 1e-05
LEARN_RATE = 0.02
BETA_ONE = 0.9
BETA_TWO = 0.999
ADAM_EPS = 1e-08
WEIGHT_DECAY = 0.1
STEP_COUNT = 5
FLOAT_PIECES = (1, 6, 7, 9, 10, 11, 12, 13, 16)

LANES = 128
TILE = 16 * LANES
SHARED_ROWS = 16
BF16 = jnp.bfloat16
F32 = jnp.float32
ANY = pl.BlockSpec(memory_space=pl.ANY)
VMEM = pl.BlockSpec(memory_space=pltpu.VMEM)
SMEM = pl.BlockSpec(memory_space=pltpu.SMEM)


def round_up(value, multiple):
    return -(-value // multiple) * multiple


class Plan:
    def __init__(self, count, shard, shared_shard, shapes):
        self.count = count
        self.shard = shard
        self.shared_shard = shared_shard
        self.shapes = shapes
        self.rows_in = round_up(shard // LANES + 2, 8)
        self.rows = round_up(self.rows_in + 16, 16)
        self.block = self.rows + SHARED_ROWS
        self.half = self.block * 4 // 11 // 16 * 16
        self.sizes = (self.half, self.block - self.half)
        self.flat_rows = count * shard // LANES
        self.alloc_rows = round_up(((count - 1) * shard // TILE) * 16 + self.rows, 16)
        self.shared_rows = count * shared_shard // LANES
        self.bases = []
        at = 0
        for shape in shapes:
            self.bases.append(at // LANES)
            at += math.prod(shape)


def as_matrix(shape):
    return shape if len(shape) == 2 else (1, shape[0])


def split_flat(length):
    return [
        (at // LANES, slice(at, min(at + LANES, length)), min(LANES, length - at))
        for at in range(0, length, LANES)
    ]


def shift_body(plan, where_ref, x_ref, s_ref, a_ref, b_ref, rows_scr, scr):
    low, row, low_shared = where_ref[0], where_ref[1], where_ref[2]
    rows_in, rows = plan.rows_in, plan.rows
    whole = plan.shard // 1024

    def load(at, carry):
        part = x_ref[0, :, pl.ds(pl.multiple_of(at * 1024, 1024), 1024)]
        rows_scr[pl.ds(pl.multiple_of(at * 8, 8), 8), :] = part.reshape(8, LANES)
        return carry

    lax.fori_loop(0, whole, load, 0, unroll=4)
    rows_scr[whole * 8 :, :] = jnp.zeros((rows_in - whole * 8, LANES), F32)
    for at, cols, lanes in split_flat(plan.shard):
        if at >= whole * 8:
            rows_scr[at : at + 1, 0:lanes] = x_ref[0, :, cols]
    scr[rows - 32 :, :] = jnp.zeros((32, LANES), F32)
    scr[0:16, :] = jnp.zeros((16, LANES), F32)
    lane = lax.broadcasted_iota(jnp.int32, (rows_in, LANES), 1)
    rolled = pltpu.roll(rows_scr[...], low, 1)
    scr[pl.ds(row, rows_in), :] = jnp.where(lane >= low, rolled, 0.0)
    scr[pl.ds(row + rows_in, 1), :] = jnp.zeros((1, LANES), F32)
    scr[pl.ds(row + 1, rows_in), :] += jnp.where(lane < low, rolled, 0.0)
    half = plan.half
    a_ref[...] = scr[0:half, :].astype(BF16)
    b_ref[0 : rows - half, :] = scr[half:, :].astype(BF16)
    rows_scr[0:8, :] = jnp.zeros((8, LANES), F32)
    for at, cols, lanes in split_flat(plan.shared_shard):
        rows_scr[at : at + 1, 0:lanes] = s_ref[:, cols]
    lane = lax.broadcasted_iota(jnp.int32, (8, LANES), 1)
    rolled = pltpu.roll(rows_scr[0:8, :], low_shared, 1)
    scr[0:16, :] = jnp.zeros((16, LANES), F32)
    scr[0:8, :] = jnp.where(lane >= low_shared, rolled, 0.0)
    scr[1:9, :] += jnp.where(lane < low_shared, rolled, 0.0)
    b_ref[rows - half : rows - half + 16, :] = scr[0:16, :].astype(BF16)


def shift_out(plan, where, flat, shared):
    return pl.pallas_call(
        partial(shift_body, plan),
        out_shape=[jax.ShapeDtypeStruct((size, LANES), BF16) for size in plan.sizes],
        in_specs=[SMEM, VMEM, VMEM],
        out_specs=[VMEM] * 2,
        scratch_shapes=[
            pltpu.VMEM((plan.rows_in, LANES), F32),
            pltpu.VMEM((plan.rows, LANES), F32),
        ],
        name="shift_out",
    )(where, flat, shared)


def finish_body(plan, n_in, where_ref, *refs):
    blocks = refs[:n_in]
    p_ref, m_ref, v_ref, ps_ref, ms_ref, vs_ref = refs[n_in : n_in + 6]
    outs = refs[n_in + 6 : n_in + 14]
    acc, rows_scr = refs[n_in + 14 :]
    low, row, low_shared = where_ref[0], where_ref[1], where_ref[2]
    rows_in, rows = plan.rows_in, plan.rows
    each = n_in // 2
    for at, rows_of in enumerate((slice(0, plan.half), slice(plan.half, plan.block))):
        parts = [block[...].astype(F32) for block in blocks[at * each : at * each + each]]
        acc[rows_of, :] = sum(parts[1:], parts[0])
    lane = lax.broadcasted_iota(jnp.int32, (rows_in, LANES), 1)
    back = lax.rem(LANES - low, LANES)
    first = pltpu.roll(acc[pl.ds(row, rows_in), :], back, 1)
    second = pltpu.roll(acc[pl.ds(row + 1, rows_in), :], back, 1)
    rows_scr[...] = jnp.where(lane < LANES - low, first, second)

    def update(grad, at, ins, out):
        weights, one, two = (ref[at] for ref in ins)
        for ref, value in zip(out, (grad,) + adam_update(weights, one, two, grad)):
            ref[at] = value

    main_in, main_out = (p_ref, m_ref, v_ref), outs[0:4]
    whole = plan.shard // 1024

    def step(at, carry):
        grad = rows_scr[pl.ds(pl.multiple_of(at * 8, 8), 8), :].reshape(1, 1024)
        cols = pl.ds(pl.multiple_of(at * 1024, 1024), 1024)
        update(grad, (0, slice(None), cols), main_in, main_out)
        return carry

    lax.fori_loop(0, whole, step, 0, unroll=4)
    for at, cols, lanes in split_flat(plan.shard):
        if at >= whole * 8:
            update(rows_scr[at : at + 1, 0:lanes], (0, slice(None), cols), main_in, main_out)
    lane = lax.broadcasted_iota(jnp.int32, (8, LANES), 1)
    back = lax.rem(LANES - low_shared, LANES)
    first = pltpu.roll(acc[rows : rows + 8, :], back, 1)
    second = pltpu.roll(acc[rows + 1 : rows + 9, :], back, 1)
    rows_scr[0:8, :] = jnp.where(lane < LANES - low_shared, first, second)
    for at, cols, lanes in split_flat(plan.shared_shard):
        update(
            rows_scr[at : at + 1, 0:lanes],
            (slice(None), cols),
            (ps_ref, ms_ref, vs_ref),
            outs[4:8],
        )


def finish(plan, where, blocks, flats, shareds):
    flat = jax.ShapeDtypeStruct(flats[0].shape, F32)
    shared = jax.ShapeDtypeStruct(shareds[0].shape, F32)
    return pl.pallas_call(
        partial(finish_body, plan, len(blocks)),
        out_shape=[flat] * 4 + [shared] * 4,
        in_specs=[SMEM] + [VMEM] * (len(blocks) + 6),
        out_specs=[VMEM] * 8,
        scratch_shapes=[
            pltpu.VMEM((plan.block, LANES), F32),
            pltpu.VMEM((plan.rows_in, LANES), F32),
        ],
        name="finish",
    )(where, *blocks, *flats, *shareds)


def chunked(total):
    step = total
    while step > 128 and step % 2 == 0:
        step //= 2
    return step


def largest_step(total, limit):
    return max(step for step in range(1, limit + 1) if total % step == 0)


def unpack_body(plan, n_in, idx_ref, *refs):
    ins = refs[:n_in]
    outs = refs[n_in : n_in + len(plan.shapes) + 1]
    flat, shf = refs[n_in + len(plan.shapes) + 1 :]
    full = plan.shard // TILE
    zero = jnp.zeros((16, LANES), F32)
    for at in range(plan.count):
        start = at * plan.shard // TILE * 16
        for tile in (0, full, full + 1):
            flat[start + tile * 16 : start + tile * 16 + 16, :] = zero
    shf[...] = jnp.zeros_like(shf)

    def place(first, second, owner):
        start = pl.multiple_of((owner * plan.shard) // TILE * 16, 16)
        edge = plan.half // 16
        for src, begin, end, origin in ((first, 1, edge, 0), (second, edge, full, edge)):
            step = largest_step(end - begin, 25)

            def move(k, carry, src=src, begin=begin, origin=origin, step=step):
                to = pl.multiple_of(start + begin * 16 + k * (step * 16), 16)
                frm = pl.multiple_of((begin - origin) * 16 + k * (step * 16), 16)
                flat[pl.ds(to, step * 16), :] = src[pl.ds(frm, step * 16), :].astype(F32)
                return carry

            lax.fori_loop(0, (end - begin) // step, move, 0)
        for src, at, tile in (
            (first, 0, 0),
            (second, full - edge, full),
            (second, full + 1 - edge, full + 1),
        ):
            rows = pl.ds(pl.multiple_of(start + tile * 16, 16), 16)
            flat[rows, :] += src[at * 16 : at * 16 + 16, :].astype(F32)
        rows = pl.ds((owner * plan.shared_shard) // LANES, 16)
        at = plan.rows - plan.half
        shf[rows, :] += second[at : at + 16, :].astype(F32)

    if n_in > 2:
        for at in range(plan.count):
            place(ins[2 * at], ins[2 * at + 1], idx_ref[at])
    else:
        for at in range(plan.count):
            place(ins[0].at[at], ins[1].at[at], at)
    for shape, base, out in zip(plan.shapes, plan.bases, outs):
        rows, width = as_matrix(shape)
        cols = width // LANES
        step = chunked(rows)
        for col in range(cols):
            if step == rows:
                if rows == 1:
                    part = flat[base + col : base + col + 1, :]
                else:
                    part = flat[pl.ds(base + col, rows, stride=cols), :]
                out[:, col * LANES : (col + 1) * LANES] = part.astype(out.dtype)
            else:

                def move(k, carry, col=col, base=base, cols=cols, step=step, out=out):
                    at = pl.multiple_of(k * (step * cols), 8) + (base + col)
                    part = flat[pl.ds(at, step, stride=cols), :]
                    to = pl.multiple_of(k * step, step)
                    out[pl.ds(to, step), col * LANES : (col + 1) * LANES] = part.astype(out.dtype)
                    return carry

                lax.fori_loop(0, rows // step, move, 0)
    shared_out = outs[-1]
    cols = D // LANES
    for col in range(cols):
        shared_out[:, col * LANES : (col + 1) * LANES] = shf[
            pl.ds(col, shared_out.shape[0], stride=cols), :
        ]


def unpack(plan, idx, blocks):
    outs = [
        jax.ShapeDtypeStruct(as_matrix(shape), F32 if at in FLOAT_PIECES else BF16)
        for at, shape in enumerate(plan.shapes)
    ]
    outs.append(jax.ShapeDtypeStruct((14, D), F32))
    return pl.pallas_call(
        partial(unpack_body, plan, len(blocks)),
        out_shape=outs,
        in_specs=[SMEM] + [VMEM] * len(blocks),
        out_specs=[VMEM] * len(outs),
        scratch_shapes=[
            pltpu.VMEM((plan.alloc_rows, LANES), F32),
            pltpu.VMEM((plan.shared_rows + 16, LANES), F32),
        ],
        compiler_params=pltpu.CompilerParams(vmem_limit_bytes=48 * 1024 * 1024),
        name="unpack",
    )(idx, *blocks)


def pack_body(plan, idx_ref, *refs):
    n_in = len(plan.shapes) + 1
    ins = refs[:n_in]
    outs = refs[n_in : n_in + 2 * plan.count]
    flat, shf = refs[n_in + 2 * plan.count :]
    tail = plan.flat_rows // 8 * 8
    flat[tail:, :] = jnp.zeros((plan.alloc_rows - tail, LANES), F32)
    for shape, base, src in zip(plan.shapes, plan.bases, ins):
        rows, width = as_matrix(shape)
        cols = width // LANES
        step = chunked(rows)
        for col in range(cols):
            if step == rows:
                part = src[:, col * LANES : (col + 1) * LANES].astype(F32)
                if rows == 1:
                    flat[base + col : base + col + 1, :] = part
                else:
                    flat[pl.ds(base + col, rows, stride=cols), :] = part
            else:

                def move(k, carry, col=col, base=base, cols=cols, step=step, src=src):
                    at = pl.multiple_of(k * (step * cols), 8) + (base + col)
                    frm = pl.multiple_of(k * step, step)
                    flat[pl.ds(at, step, stride=cols), :] = src[
                        pl.ds(frm, step), col * LANES : (col + 1) * LANES
                    ].astype(F32)
                    return carry

                lax.fori_loop(0, rows // step, move, 0)
    shf[...] = jnp.zeros_like(shf)
    cols = D // LANES
    for col in range(cols):
        shf[pl.ds(col, 14, stride=cols), :] = ins[-1][:, col * LANES : (col + 1) * LANES]

    half = plan.half
    for at in range(plan.count):
        owner = idx_ref[at]
        start = pl.multiple_of((owner * plan.shard) // TILE * 16, 16)
        for out, begin, end in ((outs[2 * at], 0, half), (outs[2 * at + 1], half, plan.rows)):
            step = 16 * largest_step((end - begin) // 16, 25)

            def move(k, carry, out=out, begin=begin, step=step, start=start):
                to = pl.multiple_of(k * step, 16)
                frm = pl.multiple_of(start + begin + k * step, 16)
                out[pl.ds(to, step), :] = flat[pl.ds(frm, step), :].astype(BF16)
                return carry

            lax.fori_loop(0, (end - begin) // step, move, 0)
        rows = pl.ds((owner * plan.shared_shard) // LANES, 16)
        outs[2 * at + 1][plan.rows - half : plan.block - half, :] = shf[rows, :].astype(BF16)


def pack(plan, idx, piece_grads, shared_grad):
    pieces = [
        grad.reshape(as_matrix(shape)).astype(F32 if at in FLOAT_PIECES else BF16)
        for at, (grad, shape) in enumerate(zip(piece_grads, plan.shapes))
    ]
    halves = [jax.ShapeDtypeStruct((size, LANES), BF16) for size in plan.sizes]
    return pl.pallas_call(
        partial(pack_body, plan),
        out_shape=halves * plan.count,
        in_specs=[SMEM] + [VMEM] * (len(pieces) + 1),
        out_specs=[VMEM] * (2 * plan.count),
        scratch_shapes=[
            pltpu.VMEM((plan.alloc_rows, LANES), F32),
            pltpu.VMEM((plan.shared_rows + 16, LANES), F32),
        ],
        compiler_params=pltpu.CompilerParams(vmem_limit_bytes=48 * 1024 * 1024),
        name="pack",
    )(idx, *pieces, shared_grad)


def permute(value, count, target, axis="dp"):
    return lax.ppermute(value, axis, [(at, target(at)) for at in range(count)])


def z_next(at):
    return (at + 4) % 16


def block_order(count):
    me = lax.axis_index("dp")
    if count != 16:
        return jnp.arange(count, dtype=jnp.int32)
    z, x, core = me // 4, (me // 2) % 2, me % 2
    order = []
    for back in range(4):
        for flip_x in range(2):
            for flip_core in range(2):
                order.append(
                    ((z + 4 - back) % 4) * 4 + (x ^ flip_x) * 2 + (core ^ flip_core)
                )
    return jnp.stack(order).astype(jnp.int32)


def across_core(value):
    return permute(value, 16, lambda at: at ^ 1)


def across_x(value):
    return permute(value, 16, lambda at: at ^ 2)


def along_z(value):
    return permute(value, 16, z_next)


def gather_blocks(count, own, alongside):
    if count != 16:
        return [lax.all_gather(half, "dp", axis=0) for half in own], alongside
    ring = [[half] for half in own]
    column = [[], []]
    for step in range(3):
        for part in range(2):
            upcoming, other = along_z(ring[part][-1]), across_x(ring[part][-1])
            if step == 0 and part == 0:
                upcoming, other, alongside = lax.optimization_barrier(
                    (upcoming, other, alongside)
                )
            elif part == 0:
                upcoming, other = lax.optimization_barrier((upcoming, other))
            else:
                upcoming, other, _ = lax.optimization_barrier((upcoming, other, ring[0][-1]))
            ring[part].append(upcoming)
            column[part].append(other)
    column[0].append(across_x(ring[0][3]))
    column[1].append(along_z(column[1][2]))
    blocks = []
    for step in range(4):
        for side in (ring, column):
            mine = [side[0][step], side[1][step]]
            blocks += mine + [across_core(half) for half in mine]
    return blocks, alongside


def add_blocks(*blocks):
    return sum(block.astype(F32) for block in blocks).astype(BF16)


def scatter_blocks(count, blocks):
    if count != 16:
        return [
            lax.psum_scatter(
                jnp.stack(blocks[part::2]).astype(F32), "dp", scatter_dimension=0, tiled=False
            )
            for part in range(2)
        ]

    def pair(back, flip_x, part):
        at = (back * 4 + flip_x * 2) * 2 + part
        return [blocks[at], across_core(blocks[at + 2])]

    moved = (across_x(add_blocks(*pair(1, 1, 0))), along_z(add_blocks(*pair(1, 1, 1))))
    running = [add_blocks(*pair(1, 0, 0), moved[0]), add_blocks(*pair(1, 0, 1))]
    far = [add_blocks(*pair(2, 1, 0)), add_blocks(*pair(2, 1, 1), moved[1])]
    final, before = [], moved[0]
    for back in (2, 3, 0):
        for part in range(2):
            arrived, other, before = lax.optimization_barrier(
                (along_z(running[part]), across_x(far[part]), before)
            )
            before = arrived
            if back == 0:
                final += pair(0, 0, part) + [other, arrived]
                continue
            running[part] = add_blocks(*pair(back, 0, part), other, arrived)
            far[part] = add_blocks(*pair((back + 1) % 4, 1, part))
    return final


def dp_sum(value):
    count = lax.axis_size("dp")
    bit = 1
    while bit < count:
        steps = [bit, 2 * bit, 3 * bit] if 4 * bit <= count else [bit]
        parts = [permute(value, count, lambda at, step=step: at ^ step) for step in steps]
        value = sum(parts, value)
        bit *= 4 if len(steps) == 3 else 2
    return value


def tensor_total(partial_sum):
    own = partial_sum.astype(BF16)
    other = permute(own, lax.axis_size("tensor"), lambda at: at ^ 1, "tensor")
    return own.astype(F32) + other.astype(F32)


tensor_back_total = tensor_total


def mat_product(left, right):
    return jnp.dot(left, right, preferred_element_type=jnp.float32)


def left_transposed_matmul(left, right):
    return lax.dot_general(
        left, right, (((0,), (0,)), ((), ())), preferred_element_type=jnp.float32
    )


def right_trans_product(left, right):
    return lax.dot_general(
        left, right, (((1,), (1,)), ((), ())), preferred_element_type=jnp.float32
    )


def layer_norm(values, scaling, offset):
    centred = values - jnp.mean(values, axis=-1, keepdims=True)
    spread = jnp.mean(centred * centred, axis=-1, keepdims=True)
    return centred * lax.rsqrt(spread + NORM_EPS) * (1.0 + scaling) + offset


def norm_back(values, scaling, offset, d_output):
    _, pull_back = jax.vjp(layer_norm, values, scaling, offset)
    return pull_back(d_output)


def silu_slope(values):
    sigma_vals = jax.nn.sigmoid(values)
    return sigma_vals * (1.0 + values * (1.0 - sigma_vals))


def position_table(seq_len, model_width):
    column = jnp.arange(model_width)
    freq_index = (column // 2).astype(jnp.float32)
    rates = jnp.exp(freq_index * (-2.0 * math.log(10000.0) / model_width))
    parts = 2 * seq_len // 16
    coarse = (16 * (parts // 2 - 1 - jnp.arange(parts))).astype(jnp.float32)[:, None] * rates
    fine = (15 - jnp.arange(16)).astype(jnp.float32)[:, None] * rates
    even = column % 2 == 0
    sin_c, cos_c = jnp.sin(coarse), jnp.cos(coarse)
    first, second = lax.optimization_barrier(
        (jnp.where(even, sin_c, cos_c), jnp.where(even, cos_c, -sin_c))
    )
    sin_f, cos_f = lax.optimization_barrier((jnp.sin(fine), jnp.cos(fine)))
    table = first[:, None] * cos_f[None] + second[:, None] * sin_f[None]
    return table.reshape(2 * seq_len, model_width)[: 2 * seq_len - 1].astype(jnp.bfloat16)


def piece_shapes(model_width, ff_part, att_part, chan_part, kernel_len):
    feed_list = [(model_width, ff_part), (ff_part,), (ff_part, model_width)]
    attn_list = [
        (model_width, 3 * att_part),
        (model_width, att_part),
        (att_part, model_width),
        (att_part,),
        (att_part,),
    ]
    conv_list = [
        (model_width, 2 * chan_part),
        (2 * chan_part,),
        (kernel_len, chan_part),
        (chan_part,),
        (chan_part,),
        (chan_part,),
        (chan_part, model_width),
    ]
    return feed_list + attn_list + conv_list + feed_list


def rel_shift(position):
    leading = position.shape[:-2]
    seq_len = position.shape[-2]
    span_len = position.shape[-1]
    padded = jnp.pad(position, [(0, 0)] * len(leading) + [(0, 0), (0, 1)])
    flattened = padded.reshape(leading + (seq_len * (span_len + 1),))
    flattened = flattened[..., seq_len - 1 : seq_len - 1 + seq_len * span_len]
    return flattened.reshape(leading + (seq_len, span_len))[..., :seq_len]


def rel_unshift(grad_shifted):
    leading = grad_shifted.shape[:-2]
    seq_len = grad_shifted.shape[-1]
    span_len = 2 * seq_len - 1
    widened = jnp.pad(grad_shifted, [(0, 0)] * len(leading) + [(0, 0), (0, span_len - seq_len)])
    flattened = widened.reshape(leading + (seq_len * span_len,))
    flattened = jnp.pad(flattened, [(0, 0)] * len(leading) + [(seq_len - 1, 1)])
    return flattened.reshape(leading + (seq_len, span_len + 1))[..., :span_len]


def attention_scores(query_u, query_v, keys_b, pos_rows):
    content = jnp.einsum("bihd,bjhd->bhij", query_u, keys_b, preferred_element_type=jnp.float32)
    position = jnp.einsum("bihd,rhd->bhir", query_v, pos_rows, preferred_element_type=jnp.float32)
    return (content + rel_shift(position)) * (1.0 / math.sqrt(query_u.shape[-1]))


def key_mask(seq_lengths):
    return (jnp.arange(SEQ_LEN)[None, :] < seq_lengths[:, None])[:, None, None, :]


def conv_front(valid, pre_glu, tap_weights, tap_bias):
    chan_part = pre_glu.shape[-1] // 2
    gated = pre_glu[..., :chan_part] * jax.nn.sigmoid(pre_glu[..., chan_part:]) * valid[..., None]
    kernel_len = tap_weights.shape[0]
    margin = (kernel_len - 1) // 2
    filters = tap_weights.reshape(kernel_len, 1, chan_part)
    summed = lax.conv_general_dilated(
        gated,
        filters,
        (1,),
        [(margin, kernel_len - 1 - margin)],
        dimension_numbers=("NWC", "WIO", "NWC"),
        feature_group_count=chan_part,
        precision=lax.Precision.HIGHEST,
    )
    return summed + tap_bias


def batch_apply(conv_out, gamma_vec, beta_vec, mean_vec, inv_std):
    return jax.nn.silu((conv_out - mean_vec) * inv_std * (1.0 + gamma_vec) + beta_vec)


def feed_forward(resid, w_in, b_in, w_out, scaling, offset, b_out):
    normed = layer_norm(resid, scaling, offset).astype(jnp.bfloat16)
    hidden_pre = mat_product(normed, w_in) + b_in
    hidden = jax.nn.silu(hidden_pre).astype(jnp.bfloat16)
    branch = tensor_total(mat_product(hidden, w_out)) + b_out
    return (resid + 0.5 * branch, (normed, hidden_pre, hidden))


def feed_back(d_resid, resid, saved, w_in, w_out, scaling, offset):
    normed, hidden_pre, hidden = saved
    d_branch = 0.5 * d_resid
    grad_bout = jnp.sum(d_branch, axis=0)
    branch_gradient_second = d_branch.astype(jnp.bfloat16)
    grad_wout = left_transposed_matmul(hidden, branch_gradient_second)
    d_pre = right_trans_product(branch_gradient_second, w_out) * silu_slope(hidden_pre)
    grad_bin = jnp.sum(d_pre, axis=0)
    d_pre_b = d_pre.astype(jnp.bfloat16)
    grad_win = left_transposed_matmul(normed, d_pre_b)
    d_normed = tensor_back_total(right_trans_product(d_pre_b, w_in))
    d_input, grad_scale, grad_offset = norm_back(resid, scaling, offset, d_normed)
    return (
        d_resid + d_input,
        [grad_win, grad_bin, grad_wout],
        [grad_scale, grad_offset, grad_bout],
    )


def attention_forward(resid, weights, scaling, offset, b_out, lengths, table):
    w_qkv, w_pos, w_att, bias_u, bias_v = weights
    seq_count = lengths.shape[0]
    att_part = w_att.shape[0]
    head_count = att_part // HEAD_DIM

    def to_heads(block):
        return block.reshape(seq_count, SEQ_LEN, head_count, HEAD_DIM)

    normed = layer_norm(resid, scaling, offset).astype(jnp.bfloat16)
    qkv_rows = mat_product(normed, w_qkv)
    query = qkv_rows[:, :att_part]
    query_u = to_heads((query + bias_u).astype(jnp.bfloat16))
    query_v = to_heads((query + bias_v).astype(jnp.bfloat16))
    keys_b = to_heads(qkv_rows[:, att_part : 2 * att_part].astype(jnp.bfloat16))
    values_b = to_heads(qkv_rows[:, 2 * att_part :].astype(jnp.bfloat16))
    pos_rows = (
        mat_product(table, w_pos)
        .astype(jnp.bfloat16)
        .reshape(2 * SEQ_LEN - 1, head_count, HEAD_DIM)
    )
    scores = attention_scores(query_u, query_v, keys_b, pos_rows)
    exponent = jnp.where(key_mask(lengths), jnp.exp(scores), 0.0)
    totals = jnp.sum(exponent, axis=-1)
    log_total = jnp.log(totals)
    probs = (exponent / totals[..., None]).astype(jnp.bfloat16)
    context = jnp.einsum("bhij,bjhd->bihd", probs, values_b, preferred_element_type=jnp.float32)
    context_rows_second = context.reshape(seq_count * SEQ_LEN, att_part).astype(jnp.bfloat16)
    branch = tensor_total(mat_product(context_rows_second, w_att)) + b_out
    return (
        resid + branch,
        (normed, query_u, query_v, keys_b, values_b, pos_rows, log_total, context_rows_second),
    )


def attention_back(d_resid, resid, saved, weights, scaling, offset, lengths, table):
    normed, query_u, query_v, keys_b, values_b, pos_rows, log_total, context_rows_second = saved
    w_qkv, _, w_att, _, _ = weights
    seq_count = lengths.shape[0]
    att_part = w_att.shape[0]
    rows_total = seq_count * SEQ_LEN
    scale = 1.0 / math.sqrt(HEAD_DIM)
    grad_bout = jnp.sum(d_resid, axis=0)
    branch_gradient_second = d_resid.astype(jnp.bfloat16)
    attention_weight_gradient = left_transposed_matmul(context_rows_second, branch_gradient_second)
    d_context = (
        right_trans_product(branch_gradient_second, w_att)
        .astype(jnp.bfloat16)
        .reshape(query_u.shape)
    )
    scores = attention_scores(query_u, query_v, keys_b, pos_rows)
    probs = jnp.where(key_mask(lengths), jnp.exp(scores - log_total[..., None]), 0.0)
    probs_b = probs.astype(jnp.bfloat16)
    d_values = jnp.einsum("bhij,bihd->bjhd", probs_b, d_context, preferred_element_type=jnp.float32)
    d_probs = jnp.einsum("bihd,bjhd->bhij", d_context, values_b, preferred_element_type=jnp.float32)
    row_dot = jnp.sum(probs * d_probs, axis=-1, keepdims=True)
    d_scores = (probs * (d_probs - row_dot) * scale).astype(jnp.bfloat16)
    d_query_u = jnp.einsum("bhij,bjhd->bihd", d_scores, keys_b, preferred_element_type=jnp.float32)
    d_keys = jnp.einsum("bhij,bihd->bjhd", d_scores, query_u, preferred_element_type=jnp.float32)
    d_position = rel_unshift(d_scores)
    d_query_v = jnp.einsum(
        "bhir,rhd->bihd", d_position, pos_rows, preferred_element_type=jnp.float32
    )
    d_pos_rows = jnp.einsum(
        "bhir,bihd->rhd", d_position, query_v, preferred_element_type=jnp.float32
    )
    content_bias_gradient = jnp.sum(d_query_u, axis=(0, 1)).reshape(att_part)
    position_bias_gradient = jnp.sum(d_query_v, axis=(0, 1)).reshape(att_part)
    d_query = (d_query_u + d_query_v).reshape(rows_total, att_part)
    d_qkv = jnp.concatenate(
        [d_query, d_keys.reshape(rows_total, att_part), d_values.reshape(rows_total, att_part)],
        axis=1,
    ).astype(jnp.bfloat16)
    query_key_value_weight_gradient = left_transposed_matmul(normed, d_qkv)
    position_weight_gradient = lax.dot_general(
        table.astype(jnp.float32),
        d_pos_rows.reshape(2 * SEQ_LEN - 1, att_part),
        (((0,), (0,)), ((), ())),
        precision=lax.Precision.HIGHEST,
    )
    d_normed = tensor_back_total(right_trans_product(d_qkv, w_qkv))
    d_input, grad_scale, grad_offset = norm_back(resid, scaling, offset, d_normed)
    return (
        d_resid + d_input,
        [
            query_key_value_weight_gradient,
            position_weight_gradient,
            attention_weight_gradient,
            content_bias_gradient,
            position_bias_gradient,
        ],
        [grad_scale, grad_offset, grad_bout],
    )


def conv_forward(resid, weights, scaling, offset, b_out, valid):
    w_glu, b_glu, tap_weights, tap_bias, gamma_vec, beta_vec, w_conv = weights
    seq_count = valid.shape[0]
    chan_part = w_conv.shape[0]
    normed = layer_norm(resid, scaling, offset).astype(jnp.bfloat16)
    pre_glu = (mat_product(normed, w_glu) + b_glu).reshape(seq_count, SEQ_LEN, 2 * chan_part)
    conv_out = conv_front(valid, pre_glu, tap_weights, tap_bias)
    masked = conv_out * valid[..., None]
    stats = dp_sum(
        jnp.stack(
            [
                jnp.sum(masked, axis=(0, 1)),
                jnp.sum(masked * conv_out, axis=(0, 1)),
                jnp.broadcast_to(jnp.sum(valid), (chan_part,)),
            ]
        )
    )
    first_sum, square_sum, count_all = stats[0], stats[1], stats[2]
    mean_vec = first_sum / count_all
    inv_std = lax.rsqrt(square_sum / count_all - mean_vec * mean_vec + BATCH_EPS)
    activated = (
        batch_apply(conv_out, gamma_vec, beta_vec, mean_vec, inv_std)
        .reshape(seq_count * SEQ_LEN, chan_part)
        .astype(jnp.bfloat16)
    )
    branch = tensor_total(mat_product(activated, w_conv)) + b_out
    return (resid + branch, (normed, pre_glu, conv_out, mean_vec, inv_std, count_all, activated))


def conv_back(d_resid, resid, saved, weights, scaling, offset, valid):
    normed, pre_glu, conv_out, mean_vec, inv_std, count_all, activated = saved
    w_glu, _, tap_weights, tap_bias, gamma_vec, beta_vec, w_conv = weights
    grad_bout = jnp.sum(d_resid, axis=0)
    branch_gradient_second = d_resid.astype(jnp.bfloat16)
    grad_wconv = left_transposed_matmul(activated, branch_gradient_second)
    d_act = right_trans_product(branch_gradient_second, w_conv).reshape(conv_out.shape)
    _, pull_norm = jax.vjp(batch_apply, conv_out, gamma_vec, beta_vec, mean_vec, inv_std)
    d_conv, grad_gamma, grad_beta, d_mean, d_inv = pull_norm(d_act)
    sums = dp_sum(jnp.stack([d_mean, d_inv]))
    d_mean, d_inv = sums[0], sums[1]
    d_var = -0.5 * inv_std * inv_std * inv_std * d_inv
    d_first = (d_mean - 2.0 * mean_vec * d_var) / count_all
    d_square = d_var / count_all
    d_conv = d_conv + valid[..., None] * (d_first + 2.0 * conv_out * d_square)
    _, pull_front = jax.vjp(partial(conv_front, valid), pre_glu, tap_weights, tap_bias)
    d_pre, grad_taps, grad_tbias = pull_front(d_conv)
    d_pre = d_pre.reshape(-1, d_pre.shape[-1])
    grad_bglu = jnp.sum(d_pre, axis=0)
    d_pre_b = d_pre.astype(jnp.bfloat16)
    grad_wglu = left_transposed_matmul(normed, d_pre_b)
    d_normed = tensor_back_total(right_trans_product(d_pre_b, w_glu))
    d_input, grad_scale, grad_offset = norm_back(resid, scaling, offset, d_normed)
    return (
        d_resid + d_input,
        [grad_wglu, grad_bglu, grad_taps, grad_tbias, grad_gamma, grad_beta, grad_wconv],
        [grad_scale, grad_offset, grad_bout],
    )


def layer_forward(resid, pieces, vectors, lengths, valid, table):
    resid_a, keep_a = feed_forward(
        resid, pieces[0], pieces[1], pieces[2], vectors[0], vectors[1], vectors[2]
    )
    resid_b, keep_b = attention_forward(
        resid_a, pieces[3:8], vectors[3], vectors[4], vectors[5], lengths, table
    )
    resid_c, keep_c = conv_forward(resid_b, pieces[8:15], vectors[6], vectors[7], vectors[8], valid)
    resid_d, keep_d = feed_forward(
        resid_c, pieces[15], pieces[16], pieces[17], vectors[9], vectors[10], vectors[11]
    )
    output = layer_norm(resid_d, vectors[12], vectors[13])
    return (output, (resid, resid_a, resid_b, resid_c, resid_d), (keep_a, keep_b, keep_c, keep_d))


def layer_back(d_output, pieces, vectors, lengths, valid, table, resids, keeps):
    resid, resid_a, resid_b, resid_c, resid_d = resids
    d_resid_d, grad_fscale, grad_foffset = norm_back(resid_d, vectors[12], vectors[13], d_output)
    d_resid_c, grads_d, shared_d = feed_back(
        d_resid_d, resid_c, keeps[3], pieces[15], pieces[17], vectors[9], vectors[10]
    )
    d_resid_b, grads_c, shared_c = conv_back(
        d_resid_c, resid_b, keeps[2], pieces[8:15], vectors[6], vectors[7], valid
    )
    d_resid_a, grads_b, shared_b = attention_back(
        d_resid_b, resid_a, keeps[1], pieces[3:8], vectors[3], vectors[4], lengths, table
    )
    d_resid, grads_a, shared_a = feed_back(
        d_resid_a, resid, keeps[0], pieces[0], pieces[2], vectors[0], vectors[1]
    )
    piece_grads = grads_a + grads_b + grads_c + grads_d
    vector_grads = shared_a + shared_b + shared_c + shared_d + [grad_fscale, grad_foffset]
    return (d_resid, piece_grads, vector_grads)


def adam_update(weights, first, second, gradient_list):
    first_new = BETA_ONE * first + (1.0 - BETA_ONE) * gradient_list
    second_new = BETA_TWO * second + (1.0 - BETA_TWO) * gradient_list * gradient_list
    first_hat = first_new / (1.0 - BETA_ONE**STEP_COUNT)
    second_hat = second_new / (1.0 - BETA_TWO**STEP_COUNT)
    weights_new = weights - LEARN_RATE * (
        first_hat / (jnp.sqrt(second_hat) + ADAM_EPS) + WEIGHT_DECAY * weights
    )
    return (weights_new, first_new, second_new)


def local(
    tokens,
    lengths,
    cotangent,
    params,
    shared,
    first_moment,
    second_moment,
    first_shared,
    second_shared,
):
    part_count = lax.axis_size("tensor")
    shapes = piece_shapes(
        D, FF // part_count, HEADS * HEAD_DIM // part_count, D // part_count, KERNEL
    )
    count = lax.axis_size("dp")
    plan = Plan(count, params.shape[2], shared.shape[1], shapes)
    me = lax.axis_index("dp")
    start = me * plan.shard % TILE
    where = jnp.stack([start % LANES, start // LANES, me * plan.shared_shard % LANES]).astype(
        jnp.int32
    )
    order = block_order(count)
    own = shift_out(plan, where, params.reshape(1, 1, -1), shared)
    table = position_table(SEQ_LEN, D)
    gathered, table = gather_blocks(count, own, table)
    unpacked = unpack(plan, order, gathered)
    pieces = [piece.reshape(shape) for piece, shape in zip(unpacked[:-1], shapes)]
    vectors = [unpacked[-1][at] for at in range(14)]
    valid = (jnp.arange(SEQ_LEN)[None, :] < lengths[:, None]).astype(F32)
    resid = tokens.astype(F32)
    result, resids, keeps = layer_forward(resid, pieces, vectors, lengths, valid, table)
    d_resid, piece_grads, vector_grads = layer_back(
        cotangent, pieces, vectors, lengths, valid, table, resids, keeps
    )
    blocks = pack(plan, order, piece_grads, jnp.stack(vector_grads))
    (
        grad_params,
        new_params,
        new_first,
        new_second,
        grad_shared,
        new_shared,
        new_first_sh,
        new_second_sh,
    ) = finish(
        plan,
        where,
        scatter_blocks(count, blocks),
        (params, first_moment, second_moment),
        (shared, first_shared, second_shared),
    )
    return (
        result,
        d_resid,
        grad_params,
        grad_shared,
        new_params,
        new_shared,
        new_first,
        new_second,
        new_first_sh,
        new_second_sh,
    )


def solution(mesh):
    in_specs = (
        P("dp", None),
        P("dp"),
        P("dp", None),
        P(None, "tensor", "dp"),
        P(None, "dp"),
        P(None, "tensor", "dp"),
        P(None, "tensor", "dp"),
        P(None, "dp"),
        P(None, "dp"),
    )
    out_specs = (
        P("dp", None),
        P("dp", None),
        P(None, "tensor", "dp"),
        P(None, "dp"),
        P(None, "tensor", "dp"),
        P(None, "dp"),
        P(None, "tensor", "dp"),
        P(None, "tensor", "dp"),
        P(None, "dp"),
        P(None, "dp"),
    )
    return jax.shard_map(local, mesh=mesh, in_specs=in_specs, out_specs=out_specs, check_vma=False)
```

profile of v0, /device:TPU:0, one launch (start us, length us, event | category | flops | bytes accessed | tf_op | source)
XLA Modules:
  0.0 259.3 jit_solution(14152278241167576622)
XLA Ops:
  1.4 2.7 %shift_out.1 = (bf16[576,128]{1,0:T(8,128)(2,1)}, bf16[1008,128]{1,0:T(8,128)(2,1)}) custom-call(s32[3]{0:T(128)} %pad_add_fusion.1.where_ref, f32[1,1,197344]{2,1,0:T(1,128)} %refs_8_.1, f32[1,448]{1,0:T(1,128)} %refs_11_.1), custom_call_target="tpu_custom_call" | custom-call | tf_op jit(solution)/shard_map/shift_out/pallas_call | solution.py:113
  4.1 3.0 %collective-permute-start.3 = (bf16[576,128]{1,0:T(8,128)(2,1)}, bf16[576,128]{1,0:T(8,128)(2,1)S(1)}, u32[]{:S(2)}, u32[]{:S(2)}) collective-permute-start(bf16[576,128]{1,0:T(8,128)(2,1)} %get-tuple-element.100.refs_0_), channel_id=1, source_target_pairs={{0,4},{2,6},{4,0},{6,2},{8,12},{10,14},{12,8},{14,10},{16,20},{18,... | collective-permute-start | bytes 442376 | tf_op jit(solution)/shard_map/ppermute | solution.py:366
  11.8 3.9 %collective-permute-done.2.refs_8_ = bf16[576,128]{1,0:T(8,128)(2,1)S(1)} collective-permute-done((bf16[576,128]{1,0:T(8,128)(2,1)}, bf16[576,128]{1,0:T(8,128)(2,1)S(1)}, u32[]{:S(2)}, u32[]{:S(2)}) %collective-permute-start.2) | collective-permute-done | bytes 147488 | tf_op jit(solution)/shard_map/ppermute | solution.py:366
  16.7 3.3 %collective-permute-done.4.refs_9_ = bf16[1008,128]{1,0:T(8,128)(2,1)S(1)} collective-permute-done((bf16[1008,128]{1,0:T(8,128)(2,1)}, bf16[1008,128]{1,0:T(8,128)(2,1)S(1)}, u32[]{:S(2)}, u32[]{:S(2)}) %collective-permute-start.4) | collective-permute-done | bytes 258080 | tf_op jit(solution)/shard_map/ppermute | solution.py:366
  23.3 6.8 %collective-permute-done.11.refs_12_ = bf16[576,128]{1,0:T(8,128)(2,1)S(1)} collective-permute-done((bf16[576,128]{1,0:T(8,128)(2,1)S(1)}, bf16[576,128]{1,0:T(8,128)(2,1)S(1)}, u32[]{:S(2)}, u32[]{:S(2)}) %collective-permute-start.11) | collective-permute-done | bytes 147488 | tf_op jit(solution)/shard_map/ppermute | solution.py:366
  30.1 2.1 collective-permute-done.10.refs_16_
  35.0 3.0 %collective-permute-done.19.refs_20_ = bf16[576,128]{1,0:T(8,128)(2,1)S(1)} collective-permute-done((bf16[576,128]{1,0:T(8,128)(2,1)S(1)}, bf16[576,128]{1,0:T(8,128)(2,1)S(1)}, u32[]{:S(2)}, u32[]{:S(2)}) %collective-permute-start.19) | collective-permute-done | bytes 147488 | tf_op jit(solution)/shard_map/ppermute | solution.py:366
  38.6 8.9 %collective-permute-done.18.refs_24_ = bf16[576,128]{1,0:T(8,128)(2,1)S(1)} collective-permute-done((bf16[576,128]{1,0:T(8,128)(2,1)S(1)}, bf16[576,128]{1,0:T(8,128)(2,1)S(1)}, u32[]{:S(2)}, u32[]{:S(2)}) %collective-permute-start.18) | collective-permute-done | bytes 147488 | tf_op jit(solution)/shard_map/ppermute | solution.py:366
  61.7 6.5 %collective-permute-done.27.refs_29_ = bf16[1008,128]{1,0:T(8,128)(2,1)} collective-permute-done((bf16[1008,128]{1,0:T(8,128)(2,1)S(1)}, bf16[1008,128]{1,0:T(8,128)(2,1)}, u32[]{:S(2)}, u32[]{:S(2)}) %collective-permute-start.27) | collective-permute-done | bytes 258080 | tf_op jit(solution)/shard_map/ppermute | solution.py:366
  83.7 8.3 %unpack.1 = (bf16[512,1024]{1,0:T(8,128)(2,1)}, f32[1,1024]{1,0:T(1,128)S(1)}, bf16[1024,512]{1,0:T(8,128)(2,1)}, bf16[512,768]{1,0:T(8,128)(2,1)}, bf16[512,256...) custom-call(s32[16]{0:T(128)S(1)} %stack.120.idx_ref, ...), custom_call_target="tpu_custom_call" | custom-call | tf_op jit(solution)/shard_map/unpack/pallas_call | solution.py:279
  92.1 1.7 convolution_add_fusion.1
  96.5 3.7 %collective-permute-done.30 = bf16[128,512]{1,0:T(8,128)(2,1)S(1)} collective-permute-done((bf16[128,512]{1,0:T(8,128)(2,1)S(1)}, bf16[128,512]{1,0:T(8,128)(2,1)S(1)}, u32[]{:S(2)}, u32[]{:S(2)}) %collective-permute-start.30) | collective-permute-done | bytes 131104 | tf_op jit(solution)/shard_map/ppermute | solution.py:366
  107.3 2.1 collective-permute-done.31
  115.8 4.3 %collective-permute-start.35 = (f32[3,256]{1,0:T(4,128)S(1)}, f32[3,256]{1,0:T(4,128)S(1)}, u32[]{:S(2)}, u32[]{:S(2)}) collective-permute-start(f32[3,256]{1,0:T(4,128)S(1)} %add_add_fusion.12), channel_id=1, source_target_pairs={{0,8},{2,10},{4,12},{6,14},{8,0},{10,2},{12,4},{14,6},{16,24},{18,... | collective-permute-start | bytes 9224 | tf_op jit(solution)/shard_map/ppermute | solution.py:366
  123.5 3.4 %collective-permute-done.38 = bf16[128,512]{1,0:T(8,128)(2,1)S(1)} collective-permute-done((bf16[128,512]{1,0:T(8,128)(2,1)S(1)}, bf16[128,512]{1,0:T(8,128)(2,1)S(1)}, u32[]{:S(2)}, u32[]{:S(2)}) %collective-permute-start.38) | collective-permute-done | bytes 131104 | tf_op jit(solution)/shard_map/ppermute | solution.py:366
  128.7 1.6 collective-permute-start.39
  130.3 3.4 %collective-permute-done.39 = bf16[128,512]{1,0:T(8,128)(2,1)S(1)} collective-permute-done((bf16[128,512]{1,0:T(8,128)(2,1)S(1)}, bf16[128,512]{1,0:T(8,128)(2,1)S(1)}, u32[]{:S(2)}, u32[]{:S(2)}) %collective-permute-start.39) | collective-permute-done | bytes 131104 | tf_op jit(solution)/shard_map/ppermute | solution.py:366
  139.3 1.9 collective-permute-done.40
  145.9 2.4 collective-permute-start.46
  153.2 2.9 %fusion.48 = f32[31,1,256]{2,1,0:T(1,128)S(1)} fusion(f32[1,128,256]{2,1,0:T(8,128)S(1)} %get-tuple-element.218, f32[1,128,256]{2,1,0:T(8,128)S(1)} %multiply_multiply_fusion.1), kind=kOutput, calls=%fused_computation.164 | convolution fusion | flops 11452416 | bytes 293888 | tf_op jit(solution)/shard_map/transpose(jvp())/conv_general_dilated | solution.py:589
  160.0 2.2 collective-permute-done.47
  171.8 2.5 collective-permute-done.48
  180.5 1.9 collective-permute-done.49
  183.0 10.3 %pack.1 = (bf16[576,128]{1,0:T(8,128)(2,1)S(1)}, bf16[1008,128]{1,0:T(8,128)(2,1)S(1)}, bf16[576,128]{1,0:T(8,128)(2,1)S(1)}, bf16[1008,128]{1,0:T(8,128)(2,1)S(...) custom-call(s32[16]{0:T(128)S(1)} %stack.120.idx_ref, ...), custom_call_target="tpu_custom_call" | custom-call | tf_op jit(solution)/shard_map/pack/pallas_call | solution.py:351
  199.8 7.6 %collective-permute-done.66 = bf16[1008,128]{1,0:T(8,128)(2,1)S(1)} collective-permute-done((bf16[1008,128]{1,0:T(8,128)(2,1)S(1)}, bf16[1008,128]{1,0:T(8,128)(2,1)S(1)}, u32[]{:S(2)}, u32[]{:S(2)}) %collective-permute-start.66) | collective-permute-done | bytes 258080 | tf_op jit(solution)/shard_map/ppermute | solution.py:366
  210.5 3.7 %collective-permute-done.58 = bf16[576,128]{1,0:T(8,128)(2,1)S(1)} collective-permute-done((bf16[576,128]{1,0:T(8,128)(2,1)S(1)}, bf16[576,128]{1,0:T(8,128)(2,1)S(1)}, u32[]{:S(2)}, u32[]{:S(2)}) %collective-permute-start.58) | collective-permute-done | bytes 147488 | tf_op jit(solution)/shard_map/ppermute | solution.py:366
  214.2 7.0 %collective-permute-done.56 = bf16[576,128]{1,0:T(8,128)(2,1)S(1)} collective-permute-done((bf16[576,128]{1,0:T(8,128)(2,1)S(1)}, bf16[576,128]{1,0:T(8,128)(2,1)S(1)}, u32[]{:S(2)}, u32[]{:S(2)}) %collective-permute-start.56) | collective-permute-done | bytes 147488 | tf_op jit(solution)/shard_map/ppermute | solution.py:366
  224.2 4.2 %collective-permute-done.61 = bf16[576,128]{1,0:T(8,128)(2,1)S(1)} collective-permute-done((bf16[576,128]{1,0:T(8,128)(2,1)S(1)}, bf16[576,128]{1,0:T(8,128)(2,1)S(1)}, u32[]{:S(2)}, u32[]{:S(2)}) %collective-permute-start.61) | collective-permute-done | bytes 147488 | tf_op jit(solution)/shard_map/ppermute | solution.py:366
  228.4 8.1 %collective-permute-done.59 = bf16[576,128]{1,0:T(8,128)(2,1)S(1)} collective-permute-done((bf16[576,128]{1,0:T(8,128)(2,1)S(1)}, bf16[576,128]{1,0:T(8,128)(2,1)S(1)}, u32[]{:S(2)}, u32[]{:S(2)}) %collective-permute-start.59) | collective-permute-done | bytes 147488 | tf_op jit(solution)/shard_map/ppermute | solution.py:366
  239.4 4.4 %collective-permute-done.70.refs_2_ = bf16[576,128]{1,0:T(8,128)(2,1)S(1)} collective-permute-done((bf16[576,128]{1,0:T(8,128)(2,1)S(1)}, bf16[576,128]{1,0:T(8,128)(2,1)S(1)}, u32[]{:S(2)}, u32[]{:S(2)}) %collective-permute-start.70) | collective-permute-done | bytes 147488 | tf_op jit(solution)/shard_map/ppermute | solution.py:366
  244.7 7.2 %collective-permute-done.68.refs_3_ = bf16[576,128]{1,0:T(8,128)(2,1)S(1)} collective-permute-done((bf16[576,128]{1,0:T(8,128)(2,1)S(1)}, bf16[576,128]{1,0:T(8,128)(2,1)S(1)}, u32[]{:S(2)}, u32[]{:S(2)}) %collective-permute-start.68) | collective-permute-done | bytes 147488 | tf_op jit(solution)/shard_map/ppermute | solution.py:366
  252.9 6.2 %finish.1 = (f32[1,1,197344]{2,1,0:T(1,128)}, f32[1,1,197344]{2,1,0:T(1,128)}, f32[1,1,197344]{2,1,0:T(1,128)}, f32[1,1,197344]{2,1,0:T(1,128)}, f32[1,448]{1,0:...) custom-call(s32[3]{0:T(128)} %pad_add_fusion.1.where_ref, bf16[576,128]{1,0:T(8,128)(2,1)} %copy-done.33, ...), custom_call_target="tpu_custom_call" | custom-call | tf_op jit(solution)/shard_map/finish/pallas_call | solution.py:178
  (425 shorter events, 114.8 us)
Async XLA Ops:
  7.0 8.7 %collective-permute-start.2 = (bf16[576,128]{1,0:T(8,128)(2,1)}, bf16[576,128]{1,0:T(8,128)(2,1)S(1)}, u32[]{:S(2)}, u32[]{:S(2)}) collective-permute-start(bf16[576,128]{1,0:T(8,128)(2,1)} %get-tuple-element.100.refs_0_), channel_id=1, source_target_pairs={{0,8},{2,10},{4,12},{6,14},{8,16},{10,18},{12,20},{14,22},{16,24},... | collective-permute-start | bytes 442376 | tf_op jit(solution)/shard_map/ppermute | solution.py:366
  9.2 10.8 %collective-permute-start.4 = (bf16[1008,128]{1,0:T(8,128)(2,1)}, bf16[1008,128]{1,0:T(8,128)(2,1)S(1)}, u32[]{:S(2)}, u32[]{:S(2)}) collective-permute-start(bf16[1008,128]{1,0:T(8,128)(2,1)} %get-tuple-element.101.refs_1_), channel_id=1, source_target_pairs={{0,8},{2,10},{4,12},{6,14},{8,16},{10,18},{12,20},{14,22},{16,24},... | collective-permute-start | bytes 774152 | tf_op jit(solution)/shard_map/ppermute | solution.py:366
  20.0 13.6 %collective-permute-start.13 = (bf16[1008,128]{1,0:T(8,128)(2,1)S(1)}, bf16[1008,128]{1,0:T(8,128)(2,1)S(1)}, u32[]{:S(2)}, u32[]{:S(2)}) collective-permute-start(bf16[1008,128]{1,0:T(8,128)(2,1)S(1)} %collective-permute-done.4.refs_9_), channel_id=1, source_target_pairs={{0,4},{2,6},{4,0},{6,2},{8,12},{10,14},{12,8},{14,10},{16,20},{18,... | collective-permute-start | bytes 774152 | tf_op jit(solution)/shard_map/ppermute | solution.py:366
  20.5 13.1 %collective-permute-start.12 = (bf16[1008,128]{1,0:T(8,128)(2,1)S(1)}, bf16[1008,128]{1,0:T(8,128)(2,1)S(1)}, u32[]{:S(2)}, u32[]{:S(2)}) collective-permute-start(bf16[1008,128]{1,0:T(8,128)(2,1)S(1)} %collective-permute-done.4.refs_9_), channel_id=1, source_target_pairs={{0,8},{2,10},{4,12},{6,14},{8,16},{10,18},{12,20},{14,22},{16,24},... | collective-permute-start | bytes 774152 | tf_op jit(solution)/shard_map/ppermute | solution.py:366
  20.5 9.5 %collective-permute-start.11 = (bf16[576,128]{1,0:T(8,128)(2,1)S(1)}, bf16[576,128]{1,0:T(8,128)(2,1)S(1)}, u32[]{:S(2)}, u32[]{:S(2)}) collective-permute-start(bf16[576,128]{1,0:T(8,128)(2,1)S(1)} %collective-permute-done.2.refs_8_), channel_id=1, source_target_pairs={{0,4},{2,6},{4,0},{6,2},{8,12},{10,14},{12,8},{14,10},{16,20},{18,... | collective-permute-start | bytes 442376 | tf_op jit(solution)/shard_map/ppermute | solution.py:366
  22.0 10.2 %collective-permute-start.10 = (bf16[576,128]{1,0:T(8,128)(2,1)S(1)}, bf16[576,128]{1,0:T(8,128)(2,1)S(1)}, u32[]{:S(2)}, u32[]{:S(2)}) collective-permute-start(bf16[576,128]{1,0:T(8,128)(2,1)S(1)} %collective-permute-done.2.refs_8_), channel_id=1, source_target_pairs={{0,8},{2,10},{4,12},{6,14},{8,16},{10,18},{12,20},{14,22},{16,24},... | collective-permute-start | bytes 442376 | tf_op jit(solution)/shard_map/ppermute | solution.py:366
  23.3 11.0 %collective-permute-start = (bf16[576,128]{1,0:T(8,128)(2,1)}, bf16[576,128]{1,0:T(8,128)(2,1)S(1)}, u32[]{:S(2)}, u32[]{:S(2)}) collective-permute-start(bf16[576,128]{1,0:T(8,128)(2,1)} %get-tuple-element.100.refs_0_), channel_id=1, source_target_pairs={{0,2},{2,0},{4,6},{6,4},{8,10},{10,8},{12,14},{14,12},{16,18},{18,... | collective-permute-start | bytes 442376 | tf_op jit(solution)/shard_map/ppermute | solution.py:366
  33.6 13.9 %collective-permute-start.1 = (bf16[1008,128]{1,0:T(8,128)(2,1)}, bf16[1008,128]{1,0:T(8,128)(2,1)S(1)}, u32[]{:S(2)}, u32[]{:S(2)}) collective-permute-start(bf16[1008,128]{1,0:T(8,128)(2,1)} %get-tuple-element.101.refs_1_), channel_id=1, source_target_pairs={{0,2},{2,0},{4,6},{6,4},{8,10},{10,8},{12,14},{14,12},{16,18},{18,... | collective-permute-start | bytes 774152 | tf_op jit(solution)/shard_map/ppermute | solution.py:366
  33.6 16.4 %collective-permute-start.21 = (bf16[1008,128]{1,0:T(8,128)(2,1)S(1)}, bf16[1008,128]{1,0:T(8,128)(2,1)S(1)}, u32[]{:S(2)}, u32[]{:S(2)}) collective-permute-start(bf16[1008,128]{1,0:T(8,128)(2,1)S(1)} %collective-permute-done.12.refs_17_), channel_id=1, source_target_pairs={{0,4},{2,6},{4,0},{6,2},{8,12},{10,14},{12,8},{14,10},{16,20},{18,... | collective-permute-start | bytes 774152 | tf_op jit(solution)/shard_map/ppermute | solution.py:366
  34.3 16.9 %collective-permute-start.20 = (bf16[1008,128]{1,0:T(8,128)(2,1)S(1)}, bf16[1008,128]{1,0:T(8,128)(2,1)S(1)}, u32[]{:S(2)}, u32[]{:S(2)}) collective-permute-start(bf16[1008,128]{1,0:T(8,128)(2,1)S(1)} %collective-permute-done.12.refs_17_), channel_id=1, source_target_pairs={{0,8},{2,10},{4,12},{6,14},{8,16},{10,18},{12,20},{14,22},{16,24},... | collective-permute-start | bytes 774152 | tf_op jit(solution)/shard_map/ppermute | solution.py:366
  35.0 12.6 %collective-permute-start.18 = (bf16[576,128]{1,0:T(8,128)(2,1)S(1)}, bf16[576,128]{1,0:T(8,128)(2,1)S(1)}, u32[]{:S(2)}, u32[]{:S(2)}) collective-permute-start(bf16[576,128]{1,0:T(8,128)(2,1)S(1)} %collective-permute-done.10.refs_16_), channel_id=1, source_target_pairs={{0,8},{2,10},{4,12},{6,14},{8,16},{10,18},{12,20},{14,22},{16,24},... | collective-permute-start | bytes 442376 | tf_op jit(solution)/shard_map/ppermute | solution.py:366
  38.0 10.8 %collective-permute-start.6 = (bf16[576,128]{1,0:T(8,128)(2,1)S(1)}, bf16[576,128]{1,0:T(8,128)(2,1)S(1)}, u32[]{:S(2)}, u32[]{:S(2)}) collective-permute-start(bf16[576,128]{1,0:T(8,128)(2,1)S(1)} %collective-permute-done.3.refs_4_), channel_id=1, source_target_pairs={{0,2},{2,0},{4,6},{6,4},{8,10},{10,8},{12,14},{14,12},{16,18},{18,... | collective-permute-start | bytes 442376 | tf_op jit(solution)/shard_map/ppermute | solution.py:366
  47.5 10.2 %collective-permute-start.7 = (bf16[1008,128]{1,0:T(8,128)(2,1)S(1)}, bf16[1008,128]{1,0:T(8,128)(2,1)S(1)}, u32[]{:S(2)}, u32[]{:S(2)}) collective-permute-start(bf16[1008,128]{1,0:T(8,128)(2,1)S(1)} %collective-permute-done.5.refs_5_), channel_id=1, source_target_pairs={{0,2},{2,0},{4,6},{6,4},{8,10},{10,8},{12,14},{14,12},{16,18},{18,... | collective-permute-start | bytes 774152 | tf_op jit(solution)/shard_map/ppermute | solution.py:366
  57.7 10.4 %collective-permute-start.27 = (bf16[1008,128]{1,0:T(8,128)(2,1)S(1)}, bf16[1008,128]{1,0:T(8,128)(2,1)}, u32[]{:S(2)}, u32[]{:S(2)}) collective-permute-start(bf16[1008,128]{1,0:T(8,128)(2,1)S(1)} %collective-permute-done.21.refs_21_), channel_id=1, source_target_pairs={{0,8},{2,10},{4,12},{6,14},{8,16},{10,18},{12,20},{14,22},{16,24},... | collective-permute-start | bytes 774152 | tf_op jit(solution)/shard_map/ppermute | solution.py:366
  58.6 9.8 %collective-permute-start.17 = (bf16[1008,128]{1,0:T(8,128)(2,1)S(1)}, bf16[1008,128]{1,0:T(8,128)(2,1)S(1)}, u32[]{:S(2)}, u32[]{:S(2)}) collective-permute-start(bf16[1008,128]{1,0:T(8,128)(2,1)S(1)} %collective-permute-done.12.refs_17_), channel_id=1, source_target_pairs={{0,2},{2,0},{4,6},{6,4},{8,10},{10,8},{12,14},{14,12},{16,18},{18,... | collective-permute-start | bytes 774152 | tf_op jit(solution)/shard_map/ppermute | solution.py:366
  193.3 15.6 %collective-permute-start.53 = (bf16[576,128]{1,0:T(8,128)(2,1)S(1)}, bf16[576,128]{1,0:T(8,128)(2,1)S(1)}, u32[]{:S(2)}, u32[]{:S(2)}) collective-permute-start(bf16[576,128]{1,0:T(8,128)(2,1)S(1)} %get-tuple-element.145), channel_id=1, source_target_pairs={{0,2},{2,0},{4,6},{6,4},{8,10},{10,8},{12,14},{14,12},{16,18},{18,... | collective-permute-start | bytes 442376 | tf_op jit(solution)/shard_map/ppermute | solution.py:366
  196.9 25.5 %collective-permute-start.71 = (bf16[1008,128]{1,0:T(8,128)(2,1)S(1)}, bf16[1008,128]{1,0:T(8,128)(2,1)S(1)}, u32[]{:S(2)}, u32[]{:S(2)}) collective-permute-start(bf16[1008,128]{1,0:T(8,128)(2,1)S(1)} %get-tuple-element.166), channel_id=1, source_target_pairs={{0,2},{2,0},{4,6},{6,4},{8,10},{10,8},{12,14},{14,12},{16,18},{18,... | collective-permute-start | bytes 774152 | tf_op jit(solution)/shard_map/ppermute | solution.py:366
  197.2 10.2 %collective-permute-start.66 = (bf16[1008,128]{1,0:T(8,128)(2,1)S(1)}, bf16[1008,128]{1,0:T(8,128)(2,1)S(1)}, u32[]{:S(2)}, u32[]{:S(2)}) collective-permute-start(bf16[1008,128]{1,0:T(8,128)(2,1)S(1)} %add_convert_fusion.6), channel_id=1, source_target_pairs={{0,8},{2,10},{4,12},{6,14},{8,16},{10,18},{12,20},{14,22},{16,24},... | collective-permute-start | bytes 774152 | tf_op jit(solution)/shard_map/ppermute | solution.py:366
  198.3 11.6 %collective-permute-start.73 = (bf16[1008,128]{1,0:T(8,128)(2,1)S(1)}, bf16[1008,128]{1,0:T(8,128)(2,1)S(1)}, u32[]{:S(2)}, u32[]{:S(2)}) collective-permute-start(bf16[1008,128]{1,0:T(8,128)(2,1)S(1)} %copy-done.70), channel_id=1, source_target_pairs={{0,2},{2,0},{4,6},{6,4},{8,10},{10,8},{12,14},{14,12},{16,18},{18,... | collective-permute-start | bytes 774152 | tf_op jit(solution)/shard_map/ppermute | solution.py:366
  198.4 10.6 %collective-permute-start.55 = (bf16[576,128]{1,0:T(8,128)(2,1)S(1)}, bf16[576,128]{1,0:T(8,128)(2,1)S(1)}, u32[]{:S(2)}, u32[]{:S(2)}) collective-permute-start(bf16[576,128]{1,0:T(8,128)(2,1)S(1)} %add_convert_fusion.14), channel_id=1, source_target_pairs={{0,4},{2,6},{4,0},{6,2},{8,12},{10,14},{12,8},{14,10},{16,20},{18,... | collective-permute-start | bytes 442376 | tf_op jit(solution)/shard_map/ppermute | solution.py:366
  208.9 12.3 %collective-permute-start.63 = (bf16[1008,128]{1,0:T(8,128)(2,1)S(1)}, bf16[1008,128]{1,0:T(8,128)(2,1)S(1)}, u32[]{:S(2)}, u32[]{:S(2)}) collective-permute-start(bf16[1008,128]{1,0:T(8,128)(2,1)S(1)} %add_convert_fusion.7), channel_id=1, source_target_pairs={{0,8},{2,10},{4,12},{6,14},{8,16},{10,18},{12,20},{14,22},{16,24},... | collective-permute-start | bytes 774152 | tf_op jit(solution)/shard_map/ppermute | solution.py:366
  209.0 12.7 %collective-permute-start.67 = (bf16[1008,128]{1,0:T(8,128)(2,1)S(1)}, bf16[1008,128]{1,0:T(8,128)(2,1)S(1)}, u32[]{:S(2)}, u32[]{:S(2)}) collective-permute-start(bf16[1008,128]{1,0:T(8,128)(2,1)S(1)} %add_convert_fusion.5), channel_id=1, source_target_pairs={{0,4},{2,6},{4,0},{6,2},{8,12},{10,14},{12,8},{14,10},{16,20},{18,... | collective-permute-start | bytes 774152 | tf_op jit(solution)/shard_map/ppermute | solution.py:366
  209.8 11.4 %collective-permute-start.56 = (bf16[576,128]{1,0:T(8,128)(2,1)S(1)}, bf16[576,128]{1,0:T(8,128)(2,1)S(1)}, u32[]{:S(2)}, u32[]{:S(2)}) collective-permute-start(bf16[576,128]{1,0:T(8,128)(2,1)S(1)} %add_convert_fusion.13), channel_id=1, source_target_pairs={{0,8},{2,10},{4,12},{6,14},{8,16},{10,18},{12,20},{14,22},{16,24},... | collective-permute-start | bytes 442376 | tf_op jit(solution)/shard_map/ppermute | solution.py:366
  214.2 9.7 %collective-permute-start.52 = (bf16[576,128]{1,0:T(8,128)(2,1)S(1)}, bf16[576,128]{1,0:T(8,128)(2,1)S(1)}, u32[]{:S(2)}, u32[]{:S(2)}) collective-permute-start(bf16[576,128]{1,0:T(8,128)(2,1)S(1)} %get-tuple-element.143), channel_id=1, source_target_pairs={{0,2},{2,0},{4,6},{6,4},{8,10},{10,8},{12,14},{14,12},{16,18},{18,... | collective-permute-start | bytes 442376 | tf_op jit(solution)/shard_map/ppermute | solution.py:366
  221.2 16.6 %collective-permute-start.76 = (bf16[1008,128]{1,0:T(8,128)(2,1)S(1)}, bf16[1008,128]{1,0:T(8,128)(2,1)S(1)}, u32[]{:S(2)}, u32[]{:S(2)}) collective-permute-start(bf16[1008,128]{1,0:T(8,128)(2,1)S(1)} %get-tuple-element.176), channel_id=1, source_target_pairs={{0,2},{2,0},{4,6},{6,4},{8,10},{10,8},{12,14},{14,12},{16,18},{18,... | collective-permute-start | bytes 774152 | tf_op jit(solution)/shard_map/ppermute | solution.py:366
  222.4 14.2 %collective-permute-start.74 = (bf16[1008,128]{1,0:T(8,128)(2,1)S(1)}, bf16[1008,128]{1,0:T(8,128)(2,1)S(1)}, u32[]{:S(2)}, u32[]{:S(2)}) collective-permute-start(bf16[1008,128]{1,0:T(8,128)(2,1)S(1)} %add_convert_fusion.3), channel_id=1, source_target_pairs={{0,4},{2,6},{4,0},{6,2},{8,12},{10,14},{12,8},{14,10},{16,20},{18,... | collective-permute-start | bytes 774152 | tf_op jit(solution)/shard_map/ppermute | solution.py:366
  223.9 13.2 %collective-permute-start.72 = (bf16[1008,128]{1,0:T(8,128)(2,1)S(1)}, bf16[1008,128]{1,0:T(8,128)(2,1)S(1)}, u32[]{:S(2)}, u32[]{:S(2)}) collective-permute-start(bf16[1008,128]{1,0:T(8,128)(2,1)S(1)} %add_convert_fusion.4), channel_id=1, source_target_pairs={{0,8},{2,10},{4,12},{6,14},{8,16},{10,18},{12,20},{14,22},{16,24},... | collective-permute-start | bytes 774152 | tf_op jit(solution)/shard_map/ppermute | solution.py:366
  224.1 12.5 %collective-permute-start.59 = (bf16[576,128]{1,0:T(8,128)(2,1)S(1)}, bf16[576,128]{1,0:T(8,128)(2,1)S(1)}, u32[]{:S(2)}, u32[]{:S(2)}) collective-permute-start(bf16[576,128]{1,0:T(8,128)(2,1)S(1)} %add_convert_fusion.11), channel_id=1, source_target_pairs={{0,8},{2,10},{4,12},{6,14},{8,16},{10,18},{12,20},{14,22},{16,24},... | collective-permute-start | bytes 442376 | tf_op jit(solution)/shard_map/ppermute | solution.py:366
  228.4 23.5 %collective-permute-start.50 = (bf16[576,128]{1,0:T(8,128)(2,1)S(1)}, bf16[576,128]{1,0:T(8,128)(2,1)S(1)}, u32[]{:S(2)}, u32[]{:S(2)}) collective-permute-start(bf16[576,128]{1,0:T(8,128)(2,1)S(1)} %get-tuple-element.139), channel_id=1, source_target_pairs={{0,2},{2,0},{4,6},{6,4},{8,10},{10,8},{12,14},{14,12},{16,18},{18,... | collective-permute-start | bytes 442376 | tf_op jit(solution)/shard_map/ppermute | solution.py:366
  236.6 15.4 %collective-permute-start.75 = (bf16[1008,128]{1,0:T(8,128)(2,1)S(1)}, bf16[1008,128]{1,0:T(8,128)(2,1)S(1)}, u32[]{:S(2)}, u32[]{:S(2)}) collective-permute-start(bf16[1008,128]{1,0:T(8,128)(2,1)S(1)} %get-tuple-element.174), channel_id=1, source_target_pairs={{0,2},{2,0},{4,6},{6,4},{8,10},{10,8},{12,14},{14,12},{16,18},{18,... | collective-permute-start | bytes 774152 | tf_op jit(solution)/shard_map/ppermute | solution.py:366
  237.8 14.1 %collective-permute-start.79 = (bf16[1008,128]{1,0:T(8,128)(2,1)S(1)}, bf16[1008,128]{1,0:T(8,128)(2,1)S(1)}, u32[]{:S(2)}, u32[]{:S(2)}) collective-permute-start(bf16[1008,128]{1,0:T(8,128)(2,1)S(1)} %add_convert_fusion.1), channel_id=1, source_target_pairs={{0,4},{2,6},{4,0},{6,2},{8,12},{10,14},{12,8},{14,10},{16,20},{18,... | collective-permute-start | bytes 774152 | tf_op jit(solution)/shard_map/ppermute | solution.py:366
  239.2 12.7 %collective-permute-start.77 = (bf16[1008,128]{1,0:T(8,128)(2,1)S(1)}, bf16[1008,128]{1,0:T(8,128)(2,1)S(1)}, u32[]{:S(2)}, u32[]{:S(2)}) collective-permute-start(bf16[1008,128]{1,0:T(8,128)(2,1)S(1)} %add_convert_fusion.2), channel_id=1, source_target_pairs={{0,8},{2,10},{4,12},{6,14},{8,16},{10,18},{12,20},{14,22},{16,24},... | collective-permute-start | bytes 774152 | tf_op jit(solution)/shard_map/ppermute | solution.py:366
  (119 other events, 566.8 us)
where the time goes:
time: 260 us; the launch traced here: 259 us
  waiting for transfers between devices  108 us (42%)
  starting transfers between devices  54.7 us (21%)
  local copies, waits for them, and re-layouts  30.9 us (12%)
  Pallas kernels  27.6 us (11%)
  matrix products  25.2 us (10%)
  other arithmetic  9.99 us (4%)
  between operations  2.9 us (1%)
    ppermute x80, waiting for transfers between devices, permute(): return lax.ppermute(value, axis, [(at, target(at)) for at in range(count)])  108 us
    ppermute x80, starting transfers between devices, permute(): return lax.ppermute(value, axis, [(at, target(at)) for at in range(count)])  54.7 us
    unnamed x147, local copies, waits for them, and re-layouts  27.1 us
    dot_general x8, matrix products, left_transposed_matmul(): lax.dot_general(left, right, (((0,), (0,)), ((), ())), preferred_element_...  10.5 us
    pallas_call x1, Pallas kernels, pack(): pl.pallas_call(partial(pack_body, plan), out_shape=halves * plan.count, i...  10.3 us
    pallas_call x1, Pallas kernels, unpack(): pl.pallas_call(partial(unpack_body, plan, len(blocks)), out_shape=outs, i...  8.34 us
    pallas_call x1, Pallas kernels, finish(): pl.pallas_call(partial(finish_body, plan, len(blocks)), out_shape=[flat]...  6.2 us
  transfers between devices with their start and end apart: 80, of which 33 were waited for; matrix products, arithmetic and copies ran while one was open for 5% of the time, Pallas kernels for 0%

commit v1 on v0

--- a/solution.py
+++ b/solution.py
@@ -199,95 +199,111 @@
     return max(step for step in range(1, limit + 1) if total % step == 0)
 
 
-def unpack_body(plan, n_in, idx_ref, *refs):
+def widen(plan, first, second, owner, origin, flat):
+    full = plan.shard // TILE
+    start = pl.multiple_of((owner * plan.shard) // TILE * 16 - origin, 16)
+    edge = plan.half // 16
+    for src, begin, end, base in ((first, 1, edge, 0), (second, edge, full, edge)):
+        step = largest_step(end - begin, 25)
+
+        def move(k, carry, src=src, begin=begin, base=base, step=step):
+            to = pl.multiple_of(start + begin * 16 + k * (step * 16), 16)
+            frm = pl.multiple_of((begin - base) * 16 + k * (step * 16), 16)
+            flat[pl.ds(to, step * 16), :] = src[pl.ds(frm, step * 16), :].astype(F32)
+            return carry
+
+        lax.fori_loop(0, (end - begin) // step, move, 0)
+    for src, at, tile in (
+        (first, 0, 0),
+        (second, full - edge, full),
+        (second, full + 1 - edge, full + 1),
+    ):
+        rows = pl.ds(pl.multiple_of(start + tile * 16, 16), 16)
+        flat[rows, :] += src[at * 16 : at * 16 + 16, :].astype(F32)
+
+
+def unpack_body(plan, which, n_in, low, high, with_shared, idx_ref, *refs):
     ins = refs[:n_in]
-    outs = refs[n_in : n_in + len(plan.shapes) + 1]
-    flat, shf = refs[n_in + len(plan.shapes) + 1 :]
+    outs = refs[n_in : n_in + len(which)]
+    flat, shf = refs[-2:]
+    origin = low * plan.shard // TILE * 16
     full = plan.shard // TILE
     zero = jnp.zeros((16, LANES), F32)
-    for at in range(plan.count):
-        start = at * plan.shard // TILE * 16
+    for at in range(low, high + 1):
+        start = at * plan.shard // TILE * 16 - origin
         for tile in (0, full, full + 1):
             flat[start + tile * 16 : start + tile * 16 + 16, :] = zero
-    shf[...] = jnp.zeros_like(shf)
-
-    def place(first, second, owner):
-        start = pl.multiple_of((owner * plan.shard) // TILE * 16, 16)
-        edge = plan.half // 16
-        for src, begin, end, origin in ((first, 1, edge, 0), (second, edge, full, edge)):
-            step = largest_step(end - begin, 25)
-
-            def move(k, carry, src=src, begin=begin, origin=origin, step=step):
-                to = pl.multiple_of(start + begin * 16 + k * (step * 16), 16)
-                frm = pl.multiple_of((begin - origin) * 16 + k * (step * 16), 16)
-                flat[pl.ds(to, step * 16), :] = src[pl.ds(frm, step * 16), :].astype(F32)
-                return carry
-
-            lax.fori_loop(0, (end - begin) // step, move, 0)
-        for src, at, tile in (
-            (first, 0, 0),
-            (second, full - edge, full),
-            (second, full + 1 - edge, full + 1),
-        ):
-            rows = pl.ds(pl.multiple_of(start + tile * 16, 16), 16)
-            flat[rows, :] += src[at * 16 : at * 16 + 16, :].astype(F32)
-        rows = pl.ds((owner * plan.shared_shard) // LANES, 16)
-        at = plan.rows - plan.half
-        shf[rows, :] += second[at : at + 16, :].astype(F32)
-
-    if n_in > 2:
-        for at in range(plan.count):
-            place(ins[2 * at], ins[2 * at + 1], idx_ref[at])
-    else:
-        for at in range(plan.count):
-            place(ins[0].at[at], ins[1].at[at], at)
-    for shape, base, out in zip(plan.shapes, plan.bases, outs):
-        rows, width = as_matrix(shape)
+    for at in range(plan.count):
+        if n_in > 2:
+            owner, first, second = idx_ref[at], ins[2 * at], ins[2 * at + 1]
+        else:
+            owner, first, second = at, ins[0].at[at], ins[1].at[at]
+
+        widen(plan, first, second, owner, origin, flat)
+
+    for at, out in zip(which, outs):
+        base = plan.bases[at] - origin
+        rows, width = as_matrix(plan.shapes[at])
         cols = width // LANES
         step = chunked(rows)
         for col in range(cols):
-            if step == rows:
-                if rows == 1:
-                    part = flat[base + col : base + col + 1, :]
-                else:
-                    part = flat[pl.ds(base + col, rows, stride=cols), :]
-                out[:, col * LANES : (col + 1) * LANES] = part.astype(out.dtype)
+            span = slice(col * LANES, (col + 1) * LANES)
+            if rows == 1:
+                out[:, span] = flat[base + col : base + col + 1, :].astype(out.dtype)
+            elif step == rows:
+                out[:, span] = flat[pl.ds(base + col, rows, stride=cols), :].astype(out.dtype)
             else:
 
-                def move(k, carry, col=col, base=base, cols=cols, step=step, out=out):
-                    at = pl.multiple_of(k * (step * cols), 8) + (base + col)
-                    part = flat[pl.ds(at, step, stride=cols), :]
+                def move(k, carry, col=col, base=base, cols=cols, step=step, out=out, span=span):
+                    frm = pl.multiple_of(k * (step * cols), 8) + (base + col)
                     to = pl.multiple_of(k * step, step)
-                    out[pl.ds(to, step), col * LANES : (col + 1) * LANES] = part.astype(out.dtype)
+                    part = flat[pl.ds(frm, step, stride=cols), :]
+                    out[pl.ds(to, step), span] = part.astype(out.dtype)
                     return carry
 
                 lax.fori_loop(0, rows // step, move, 0)
-    shared_out = outs[-1]
-    cols = D // LANES
-    for col in range(cols):
-        shared_out[:, col * LANES : (col + 1) * LANES] = shf[
-            pl.ds(col, shared_out.shape[0], stride=cols), :
-        ]
-
-
-def unpack(plan, idx, blocks):
+    if with_shared:
+        shared_out = refs[-3]
+        shf[...] = jnp.zeros_like(shf)
+        for at in range(plan.count):
+            owner, second = (idx_ref[at], ins[2 * at + 1]) if n_in > 2 else (at, ins[1].at[at])
+            rows = pl.ds((owner * plan.shared_shard) // LANES, 16)
+            frm = plan.rows - plan.half
+            shf[rows, :] += second[frm : frm + 16, :].astype(F32)
+        cols = D // LANES
+        for col in range(cols):
+            shared_out[:, col * LANES : (col + 1) * LANES] = shf[pl.ds(col, 14, stride=cols), :]
+
+
+def unpack(plan, idx, blocks, which, with_shared):
+    low = plan.bases[which[0]] * LANES // plan.shard
+    last = plan.bases[which[-1]] * LANES + math.prod(plan.shapes[which[-1]]) - 1
+    high = last // plan.shard
+    rows = high * plan.shard // TILE * 16 + plan.rows - low * plan.shard // TILE * 16
     outs = [
-        jax.ShapeDtypeStruct(as_matrix(shape), F32 if at in FLOAT_PIECES else BF16)
-        for at, shape in enumerate(plan.shapes)
+        jax.ShapeDtypeStruct(as_matrix(plan.shapes[at]), F32 if at in FLOAT_PIECES else BF16)
+        for at in which
     ]
-    outs.append(jax.ShapeDtypeStruct((14, D), F32))
+    if with_shared:
+        outs.append(jax.ShapeDtypeStruct((14, D), F32))
     return pl.pallas_call(
-        partial(unpack_body, plan, len(blocks)),
+        partial(unpack_body, plan, tuple(which), len(blocks), low, high, with_shared),
         out_shape=outs,
         in_specs=[SMEM] + [VMEM] * len(blocks),
         out_specs=[VMEM] * len(outs),
         scratch_shapes=[
-            pltpu.VMEM((plan.alloc_rows, LANES), F32),
+            pltpu.VMEM((rows, LANES), F32),
             pltpu.VMEM((plan.shared_rows + 16, LANES), F32),
         ],
         compiler_params=pltpu.CompilerParams(vmem_limit_bytes=48 * 1024 * 1024),
-        name="unpack",
+        cost_estimate=pl.CostEstimate(
+            flops=0, bytes_accessed=rows * 2048, transcendentals=0
+        ),
     )(idx, *blocks)
+
+
+def largest_step(total, limit):
+    return max(step for step in range(1, limit + 1) if total % step == 0)
 
 
 def pack_body(plan, idx_ref, *refs):
@@ -366,8 +382,12 @@
     return lax.ppermute(value, axis, [(at, target(at)) for at in range(count)])
 
 
+def gray(value):
+    return value ^ (value >> 1)
+
+
 def z_next(at):
-    return (at + 4) % 16
+    return gray((gray(at // 4) + 1) % 4) * 4 + at % 4
 
 
 def block_order(count):
@@ -380,7 +400,7 @@
         for flip_x in range(2):
             for flip_core in range(2):
                 order.append(
-                    ((z + 4 - back) % 4) * 4 + (x ^ flip_x) * 2 + (core ^ flip_core)
+                    gray((gray(z) + 4 - back) % 4) * 4 + (x ^ flip_x) * 2 + (core ^ flip_core)
                 )
     return jnp.stack(order).astype(jnp.int32)
 
@@ -442,7 +462,9 @@
         at = (back * 4 + flip_x * 2) * 2 + part
         return [blocks[at], across_core(blocks[at + 2])]
 
-    moved = (across_x(add_blocks(*pair(1, 1, 0))), along_z(add_blocks(*pair(1, 1, 1))))
+    sent = [pair(1, 1, part) for part in range(2)]
+    *blocks, sent[0][1], sent[1][1] = lax.optimization_barrier((*blocks, sent[0][1], sent[1][1]))
+    moved = (across_x(add_blocks(*sent[0])), along_z(add_blocks(*sent[1])))
     running = [add_blocks(*pair(1, 0, 0), moved[0]), add_blocks(*pair(1, 0, 1))]
     far = [add_blocks(*pair(2, 1, 0)), add_blocks(*pair(2, 1, 1), moved[1])]
     final, before = [], moved[0]
@@ -475,9 +497,6 @@
     own = partial_sum.astype(BF16)
     other = permute(own, lax.axis_size("tensor"), lambda at: at ^ 1, "tensor")
     return own.astype(F32) + other.astype(F32)
-
-
-tensor_back_total = tensor_total
 
 
 def mat_product(left, right):
@@ -620,7 +639,7 @@
     grad_bin = jnp.sum(d_pre, axis=0)
     d_pre_b = d_pre.astype(jnp.bfloat16)
     grad_win = left_transposed_matmul(normed, d_pre_b)
-    d_normed = tensor_back_total(right_trans_product(d_pre_b, w_in))
+    d_normed = tensor_total(right_trans_product(d_pre_b, w_in))
     d_input, grad_scale, grad_offset = norm_back(resid, scaling, offset, d_normed)
     return (
         d_resid + d_input,
@@ -709,7 +728,7 @@
         (((0,), (0,)), ((), ())),
         precision=lax.Precision.HIGHEST,
     )
-    d_normed = tensor_back_total(right_trans_product(d_qkv, w_qkv))
+    d_normed = tensor_total(right_trans_product(d_qkv, w_qkv))
     d_input, grad_scale, grad_offset = norm_back(resid, scaling, offset, d_normed)
     return (
         d_resid + d_input,
@@ -774,7 +793,7 @@
     grad_bglu = jnp.sum(d_pre, axis=0)
     d_pre_b = d_pre.astype(jnp.bfloat16)
     grad_wglu = left_transposed_matmul(normed, d_pre_b)
-    d_normed = tensor_back_total(right_trans_product(d_pre_b, w_glu))
+    d_normed = tensor_total(right_trans_product(d_pre_b, w_glu))
     d_input, grad_scale, grad_offset = norm_back(resid, scaling, offset, d_normed)
     return (
         d_resid + d_input,
@@ -855,9 +874,9 @@
     own = shift_out(plan, where, params.reshape(1, 1, -1), shared)
     table = position_table(SEQ_LEN, D)
     gathered, table = gather_blocks(count, own, table)
-    unpacked = unpack(plan, order, gathered)
-    pieces = [piece.reshape(shape) for piece, shape in zip(unpacked[:-1], shapes)]
-    vectors = [unpacked[-1][at] for at in range(14)]
+    *unpacked, vector_rows = unpack(plan, order, gathered, range(len(shapes)), True)
+    pieces = [piece.reshape(shape) for piece, shape in zip(unpacked, shapes)]
+    vectors = [vector_rows[at] for at in range(14)]
     valid = (jnp.arange(SEQ_LEN)[None, :] < lengths[:, None]).astype(F32)
     resid = tokens.astype(F32)
     result, resids, keeps = layer_forward(resid, pieces, vectors, lengths, valid, table)

time: 260 us -> 259 us (level)
  waiting for transfers between devices: 108 us -> 89.3 us
  starting transfers between devices: 54.7 us -> 69.2 us
  other arithmetic: 9.99 us -> 12.7 us
    ppermute x80, waiting for transfers between devices: 108 us -> 89.3 us  [permute(): return lax.ppermute(value, axis, [(at, target(at)) for at in range(count)])]
    ppermute x80, starting transfers between devices: 54.7 us -> 69.2 us  [permute(): return lax.ppermute(value, axis, [(at, target(at)) for at in range(count)])]
    unnamed x147 -> x183, local copies, waits for them, and re-layouts: 27.1 us -> 28 us
  transfers between devices with their start and end apart: 80 -> 80, of which waited for: 33 -> 32; matrix products, arithmetic and copies ran while one was open for 5% -> 5% of each run, Pallas kernels for 0% -> 0%
where the time goes in v1:
time: 259 us; the launch traced here: 258 us
  waiting for transfers between devices  89.3 us (34%)
  starting transfers between devices  69.2 us (27%)
  local copies, waits for them, and re-layouts  31.9 us (12%)
  Pallas kernels  27.5 us (11%)
  matrix products  25 us (10%)
  other arithmetic  12.7 us (5%)
  between operations  2.89 us (1%)
    ppermute x80, waiting for transfers between devices, permute(): return lax.ppermute(value, axis, [(at, target(at)) for at in range(count)])  89.3 us
    ppermute x80, starting transfers between devices, permute(): return lax.ppermute(value, axis, [(at, target(at)) for at in range(count)])  69.2 us
    unnamed x183, local copies, waits for them, and re-layouts  28 us
    dot_general x8, matrix products, left_transposed_matmul(): lax.dot_general(left, right, (((0,), (0,)), ((), ())), preferred_element_...  10.5 us
    pallas_call x1, Pallas kernels, pack(): pl.pallas_call(partial(pack_body, plan), out_shape=halves * plan.count, i...  10.3 us
    pallas_call x1, Pallas kernels, unpack(): pl.pallas_call(partial(unpack_body, plan, tuple(which), len(blocks), low,...  8.3 us
    pallas_call x1, Pallas kernels, finish(): pl.pallas_call(partial(finish_body, plan, len(blocks)), out_shape=[flat]...  6.2 us
  transfers between devices with their start and end apart: 80, of which 32 were waited for; matrix products, arithmetic and copies ran while one was open for 5% of the time, Pallas kernels for 0%

profile of v1, /device:TPU:0, one launch (start us, length us, event | category | flops | bytes accessed | tf_op | source)
XLA Modules:
  0.0 258.5 jit_solution(7957229725579830062)
XLA Ops:
  1.3 2.7 %shift_out.1 = (bf16[576,128]{1,0:T(8,128)(2,1)}, bf16[1008,128]{1,0:T(8,128)(2,1)}) custom-call(s32[3]{0:T(128)} %pad_add_fusion.1.where_ref, f32[1,1,197344]{2,1,0:T(1,128)} %refs_8_.1, f32[1,448]{1,0:T(1,128)} %refs_11_.1), custom_call_target="tpu_custom_call" | custom-call | tf_op jit(solution)/shard_map/shift_out/pallas_call | solution.py:113
  4.0 3.0 %collective-permute-start.3 = (bf16[576,128]{1,0:T(8,128)(2,1)}, bf16[576,128]{1,0:T(8,128)(2,1)S(1)}, u32[]{:S(2)}, u32[]{:S(2)}) collective-permute-start(bf16[576,128]{1,0:T(8,128)(2,1)} %get-tuple-element.130.refs_0_), channel_id=1, source_target_pairs={{0,4},{2,6},{4,0},{6,2},{8,12},{10,14},{12,8},{14,10},{16,20},{18,... | collective-permute-start | bytes 442376 | tf_op jit(solution)/shard_map/ppermute | solution.py:382
  9.1 2.6 %collective-permute-start.4 = (bf16[1008,128]{1,0:T(8,128)(2,1)}, bf16[1008,128]{1,0:T(8,128)(2,1)S(1)}, u32[]{:S(2)}, u32[]{:S(2)}) collective-permute-start(bf16[1008,128]{1,0:T(8,128)(2,1)} %get-tuple-element.131.refs_1_), channel_id=1, source_target_pairs={{0,8},{2,10},{4,12},{6,14},{8,24},{10,26},{12,28},{14,30},{16,0},{... | collective-permute-start | bytes 774152 | tf_op jit(solution)/shard_map/ppermute | solution.py:382
  12.8 2.0 collective-permute-done.2.refs_8_
  16.6 2.3 collective-permute-done.4.refs_9_
  21.9 3.3 %collective-permute-start.10 = (bf16[576,128]{1,0:T(8,128)(2,1)S(1)}, bf16[576,128]{1,0:T(8,128)(2,1)S(1)}, u32[]{:S(2)}, u32[]{:S(2)}) collective-permute-start(bf16[576,128]{1,0:T(8,128)(2,1)S(1)} %collective-permute-done.2.refs_8_), channel_id=1, source_target_pairs={{0,8},{2,10},{4,12},{6,14},{8,24},{10,26},{12,28},{14,30},{16,0},{... | collective-permute-start | bytes 442376 | tf_op jit(solution)/shard_map/ppermute | solution.py:382
  25.1 3.8 %collective-permute-done.11.refs_12_ = bf16[576,128]{1,0:T(8,128)(2,1)S(1)} collective-permute-done((bf16[576,128]{1,0:T(8,128)(2,1)S(1)}, bf16[576,128]{1,0:T(8,128)(2,1)S(1)}, u32[]{:S(2)}, u32[]{:S(2)}) %collective-permute-start.11) | collective-permute-done | bytes 147488 | tf_op jit(solution)/shard_map/ppermute | solution.py:382
  33.6 3.4 %collective-permute-start.18 = (bf16[576,128]{1,0:T(8,128)(2,1)S(1)}, bf16[576,128]{1,0:T(8,128)(2,1)S(1)}, u32[]{:S(2)}, u32[]{:S(2)}) collective-permute-start(bf16[576,128]{1,0:T(8,128)(2,1)S(1)} %collective-permute-done.10.refs_16_), channel_id=1, source_target_pairs={{0,8},{2,10},{4,12},{6,14},{8,24},{10,26},{12,28},{14,30},{16,0},{... | collective-permute-start | bytes 442376 | tf_op jit(solution)/shard_map/ppermute | solution.py:382
  37.7 6.9 %collective-permute-done.18.refs_24_ = bf16[576,128]{1,0:T(8,128)(2,1)S(1)} collective-permute-done((bf16[576,128]{1,0:T(8,128)(2,1)S(1)}, bf16[576,128]{1,0:T(8,128)(2,1)S(1)}, u32[]{:S(2)}, u32[]{:S(2)}) %collective-permute-start.18) | collective-permute-done | bytes 147488 | tf_op jit(solution)/shard_map/ppermute | solution.py:382
  59.5 4.8 %collective-permute-done.27.refs_29_ = bf16[1008,128]{1,0:T(8,128)(2,1)} collective-permute-done((bf16[1008,128]{1,0:T(8,128)(2,1)S(1)}, bf16[1008,128]{1,0:T(8,128)(2,1)}, u32[]{:S(2)}, u32[]{:S(2)}) %collective-permute-start.27) | collective-permute-done | bytes 258080 | tf_op jit(solution)/shard_map/ppermute | solution.py:382
  79.9 8.3 %shard_map.168 = (bf16[512,1024]{1,0:T(8,128)(2,1)}, f32[1,1024]{1,0:T(1,128)S(1)}, bf16[1024,512]{1,0:T(8,128)(2,1)}, bf16[512,768]{1,0:T(8,128)(2,1)}, bf16[51...) custom-call(s32[16]{0:T(128)S(1)} %stack.120.idx_ref, ...), custom_call_target="tpu_custom_call" | custom-call | bytes 50561024 | tf_op jit(solution)/shard_map/pallas_call | solution.py:289
  93.1 3.6 %collective-permute-done.30 = bf16[128,512]{1,0:T(8,128)(2,1)S(1)} collective-permute-done((bf16[128,512]{1,0:T(8,128)(2,1)S(1)}, bf16[128,512]{1,0:T(8,128)(2,1)S(1)}, u32[]{:S(2)}, u32[]{:S(2)}) %collective-permute-start.30) | collective-permute-done | bytes 131104 | tf_op jit(solution)/shard_map/ppermute | solution.py:382
  104.3 2.0 collective-permute-done.31
  112.7 3.6 %collective-permute-start.37 = (f32[3,256]{1,0:T(4,128)S(1)}, f32[3,256]{1,0:T(4,128)S(1)}, u32[]{:S(2)}, u32[]{:S(2)}) collective-permute-start(f32[3,256]{1,0:T(4,128)S(1)} %add_add_fusion.12), channel_id=1, source_target_pairs={{0,24},{2,26},{4,28},{6,30},{8,16},{10,18},{12,20},{14,22},{16,8},... | collective-permute-start | bytes 9224 | tf_op jit(solution)/shard_map/ppermute | solution.py:382
  118.1 2.7 %collective-permute-done.36 = f32[3,256]{1,0:T(4,128)S(1)} collective-permute-done((f32[3,256]{1,0:T(4,128)S(1)}, f32[3,256]{1,0:T(4,128)S(1)}, u32[]{:S(2)}, u32[]{:S(2)}) %collective-permute-start.36) | collective-permute-done | bytes 3104 | tf_op jit(solution)/shard_map/ppermute | solution.py:382
  122.6 3.4 %collective-permute-done.38 = bf16[128,512]{1,0:T(8,128)(2,1)S(1)} collective-permute-done((bf16[128,512]{1,0:T(8,128)(2,1)S(1)}, bf16[128,512]{1,0:T(8,128)(2,1)S(1)}, u32[]{:S(2)}, u32[]{:S(2)}) %collective-permute-start.38) | collective-permute-done | bytes 131104 | tf_op jit(solution)/shard_map/ppermute | solution.py:382
  129.4 3.4 %collective-permute-done.39 = bf16[128,512]{1,0:T(8,128)(2,1)S(1)} collective-permute-done((bf16[128,512]{1,0:T(8,128)(2,1)S(1)}, bf16[128,512]{1,0:T(8,128)(2,1)S(1)}, u32[]{:S(2)}, u32[]{:S(2)}) %collective-permute-start.39) | collective-permute-done | bytes 131104 | tf_op jit(solution)/shard_map/ppermute | solution.py:382
  148.7 2.3 collective-permute-start.44
  152.7 2.9 %fusion.48 = f32[31,1,256]{2,1,0:T(1,128)S(1)} fusion(f32[1,128,256]{2,1,0:T(8,128)S(1)} %get-tuple-element.278, f32[1,128,256]{2,1,0:T(8,128)S(1)} %multiply_multiply_fusion.1), kind=kOutput, calls=%fused_computation.164 | convolution fusion | flops 11452416 | bytes 293888 | tf_op jit(solution)/shard_map/transpose(jvp())/conv_general_dilated | solution.py:608
  159.5 2.2 collective-permute-done.47
  171.4 2.5 collective-permute-done.48
  182.6 10.3 %pack.1 = (bf16[576,128]{1,0:T(8,128)(2,1)S(1)}, bf16[1008,128]{1,0:T(8,128)(2,1)S(1)}, bf16[576,128]{1,0:T(8,128)(2,1)S(1)}, bf16[1008,128]{1,0:T(8,128)(2,1)S(...) custom-call(s32[16]{0:T(128)S(1)} %stack.120.idx_ref, ...), custom_call_target="tpu_custom_call" | custom-call | tf_op jit(solution)/shard_map/pack/pallas_call | solution.py:367
  197.4 3.4 %collective-permute-done.56 = bf16[576,128]{1,0:T(8,128)(2,1)S(1)} collective-permute-done((bf16[576,128]{1,0:T(8,128)(2,1)S(1)}, bf16[576,128]{1,0:T(8,128)(2,1)S(1)}, u32[]{:S(2)}, u32[]{:S(2)}) %collective-permute-start.56) | collective-permute-done | bytes 147488 | tf_op jit(solution)/shard_map/ppermute | solution.py:382
  200.8 2.0 collective-permute-start.66
  204.6 4.5 %collective-permute-done.66 = bf16[1008,128]{1,0:T(8,128)(2,1)S(1)} collective-permute-done((bf16[1008,128]{1,0:T(8,128)(2,1)S(1)}, bf16[1008,128]{1,0:T(8,128)(2,1)S(1)}, u32[]{:S(2)}, u32[]{:S(2)}) %collective-permute-start.66) | collective-permute-done | bytes 258080 | tf_op jit(solution)/shard_map/ppermute | solution.py:382
  214.6 2.1 collective-permute-done.57
  216.7 4.8 %collective-permute-done.59 = bf16[576,128]{1,0:T(8,128)(2,1)S(1)} collective-permute-done((bf16[576,128]{1,0:T(8,128)(2,1)S(1)}, bf16[576,128]{1,0:T(8,128)(2,1)S(1)}, u32[]{:S(2)}, u32[]{:S(2)}) %collective-permute-start.59) | collective-permute-done | bytes 147488 | tf_op jit(solution)/shard_map/ppermute | solution.py:382
  226.4 2.4 collective-permute-done.62
  228.8 7.2 %collective-permute-done.60 = bf16[576,128]{1,0:T(8,128)(2,1)S(1)} collective-permute-done((bf16[576,128]{1,0:T(8,128)(2,1)S(1)}, bf16[576,128]{1,0:T(8,128)(2,1)S(1)}, u32[]{:S(2)}, u32[]{:S(2)}) %collective-permute-start.60) | collective-permute-done | bytes 147488 | tf_op jit(solution)/shard_map/ppermute | solution.py:382
  238.9 4.4 %collective-permute-done.70.refs_2_ = bf16[576,128]{1,0:T(8,128)(2,1)S(1)} collective-permute-done((bf16[576,128]{1,0:T(8,128)(2,1)S(1)}, bf16[576,128]{1,0:T(8,128)(2,1)S(1)}, u32[]{:S(2)}, u32[]{:S(2)}) %collective-permute-start.70) | collective-permute-done | bytes 147488 | tf_op jit(solution)/shard_map/ppermute | solution.py:382
  244.1 6.3 %collective-permute-done.68.refs_3_ = bf16[576,128]{1,0:T(8,128)(2,1)S(1)} collective-permute-done((bf16[576,128]{1,0:T(8,128)(2,1)S(1)}, bf16[576,128]{1,0:T(8,128)(2,1)S(1)}, u32[]{:S(2)}, u32[]{:S(2)}) %collective-permute-start.68) | collective-permute-done | bytes 147488 | tf_op jit(solution)/shard_map/ppermute | solution.py:382
  252.1 6.2 %finish.1 = (f32[1,1,197344]{2,1,0:T(1,128)}, f32[1,1,197344]{2,1,0:T(1,128)}, f32[1,1,197344]{2,1,0:T(1,128)}, f32[1,1,197344]{2,1,0:T(1,128)}, f32[1,448]{1,0:...) custom-call(s32[3]{0:T(128)} %pad_add_fusion.1.where_ref, bf16[576,128]{1,0:T(8,128)(2,1)} %copy-done.33, ...), custom_call_target="tpu_custom_call" | custom-call | tf_op jit(solution)/shard_map/finish/pallas_call | solution.py:178
  (461 shorter events, 130.0 us)
Async XLA Ops:
  4.0 8.8 %collective-permute-start.3 = (bf16[576,128]{1,0:T(8,128)(2,1)}, bf16[576,128]{1,0:T(8,128)(2,1)S(1)}, u32[]{:S(2)}, u32[]{:S(2)}) collective-permute-start(bf16[576,128]{1,0:T(8,128)(2,1)} %get-tuple-element.130.refs_0_), channel_id=1, source_target_pairs={{0,4},{2,6},{4,0},{6,2},{8,12},{10,14},{12,8},{14,10},{16,20},{18,... | collective-permute-start | bytes 442376 | tf_op jit(solution)/shard_map/ppermute | solution.py:382
  7.0 7.8 %collective-permute-start.2 = (bf16[576,128]{1,0:T(8,128)(2,1)}, bf16[576,128]{1,0:T(8,128)(2,1)S(1)}, u32[]{:S(2)}, u32[]{:S(2)}) collective-permute-start(bf16[576,128]{1,0:T(8,128)(2,1)} %get-tuple-element.130.refs_0_), channel_id=1, source_target_pairs={{0,8},{2,10},{4,12},{6,14},{8,24},{10,26},{12,28},{14,30},{16,0},{... | collective-permute-start | bytes 442376 | tf_op jit(solution)/shard_map/ppermute | solution.py:382
  8.6 8.0 %collective-permute-start.5 = (bf16[1008,128]{1,0:T(8,128)(2,1)}, bf16[1008,128]{1,0:T(8,128)(2,1)S(1)}, u32[]{:S(2)}, u32[]{:S(2)}) collective-permute-start(bf16[1008,128]{1,0:T(8,128)(2,1)} %get-tuple-element.131.refs_1_), channel_id=1, source_target_pairs={{0,4},{2,6},{4,0},{6,2},{8,12},{10,14},{12,8},{14,10},{16,20},{18,... | collective-permute-start | bytes 774152 | tf_op jit(solution)/shard_map/ppermute | solution.py:382
  9.1 9.9 %collective-permute-start.4 = (bf16[1008,128]{1,0:T(8,128)(2,1)}, bf16[1008,128]{1,0:T(8,128)(2,1)S(1)}, u32[]{:S(2)}, u32[]{:S(2)}) collective-permute-start(bf16[1008,128]{1,0:T(8,128)(2,1)} %get-tuple-element.131.refs_1_), channel_id=1, source_target_pairs={{0,8},{2,10},{4,12},{6,14},{8,24},{10,26},{12,28},{14,30},{16,0},{... | collective-permute-start | bytes 774152 | tf_op jit(solution)/shard_map/ppermute | solution.py:382
  19.0 12.7 %collective-permute-start.13 = (bf16[1008,128]{1,0:T(8,128)(2,1)S(1)}, bf16[1008,128]{1,0:T(8,128)(2,1)S(1)}, u32[]{:S(2)}, u32[]{:S(2)}) collective-permute-start(bf16[1008,128]{1,0:T(8,128)(2,1)S(1)} %collective-permute-done.4.refs_9_), channel_id=1, source_target_pairs={{0,4},{2,6},{4,0},{6,2},{8,12},{10,14},{12,8},{14,10},{16,20},{18,... | collective-permute-start | bytes 774152 | tf_op jit(solution)/shard_map/ppermute | solution.py:382
  19.5 12.2 %collective-permute-start.12 = (bf16[1008,128]{1,0:T(8,128)(2,1)S(1)}, bf16[1008,128]{1,0:T(8,128)(2,1)S(1)}, u32[]{:S(2)}, u32[]{:S(2)}) collective-permute-start(bf16[1008,128]{1,0:T(8,128)(2,1)S(1)} %collective-permute-done.4.refs_9_), channel_id=1, source_target_pairs={{0,8},{2,10},{4,12},{6,14},{8,24},{10,26},{12,28},{14,30},{16,0},{... | collective-permute-start | bytes 774152 | tf_op jit(solution)/shard_map/ppermute | solution.py:382
  20.5 8.4 %collective-permute-start.11 = (bf16[576,128]{1,0:T(8,128)(2,1)S(1)}, bf16[576,128]{1,0:T(8,128)(2,1)S(1)}, u32[]{:S(2)}, u32[]{:S(2)}) collective-permute-start(bf16[576,128]{1,0:T(8,128)(2,1)S(1)} %collective-permute-done.2.refs_8_), channel_id=1, source_target_pairs={{0,4},{2,6},{4,0},{6,2},{8,12},{10,14},{12,8},{14,10},{16,20},{18,... | collective-permute-start | bytes 442376 | tf_op jit(solution)/shard_map/ppermute | solution.py:382
  21.9 8.3 %collective-permute-start.10 = (bf16[576,128]{1,0:T(8,128)(2,1)S(1)}, bf16[576,128]{1,0:T(8,128)(2,1)S(1)}, u32[]{:S(2)}, u32[]{:S(2)}) collective-permute-start(bf16[576,128]{1,0:T(8,128)(2,1)S(1)} %collective-permute-done.2.refs_8_), channel_id=1, source_target_pairs={{0,8},{2,10},{4,12},{6,14},{8,24},{10,26},{12,28},{14,30},{16,0},{... | collective-permute-start | bytes 442376 | tf_op jit(solution)/shard_map/ppermute | solution.py:382
  25.1 7.8 %collective-permute-start = (bf16[576,128]{1,0:T(8,128)(2,1)}, bf16[576,128]{1,0:T(8,128)(2,1)S(1)}, u32[]{:S(2)}, u32[]{:S(2)}) collective-permute-start(bf16[576,128]{1,0:T(8,128)(2,1)} %get-tuple-element.130.refs_0_), channel_id=1, source_target_pairs={{0,2},{2,0},{4,6},{6,4},{8,10},{10,8},{12,14},{14,12},{16,18},{18,... | collective-permute-start | bytes 442376 | tf_op jit(solution)/shard_map/ppermute | solution.py:382
  31.6 13.0 %collective-permute-start.1 = (bf16[1008,128]{1,0:T(8,128)(2,1)}, bf16[1008,128]{1,0:T(8,128)(2,1)S(1)}, u32[]{:S(2)}, u32[]{:S(2)}) collective-permute-start(bf16[1008,128]{1,0:T(8,128)(2,1)} %get-tuple-element.131.refs_1_), channel_id=1, source_target_pairs={{0,2},{2,0},{4,6},{6,4},{8,10},{10,8},{12,14},{14,12},{16,18},{18,... | collective-permute-start | bytes 774152 | tf_op jit(solution)/shard_map/ppermute | solution.py:382
  31.6 15.5 %collective-permute-start.21 = (bf16[1008,128]{1,0:T(8,128)(2,1)S(1)}, bf16[1008,128]{1,0:T(8,128)(2,1)S(1)}, u32[]{:S(2)}, u32[]{:S(2)}) collective-permute-start(bf16[1008,128]{1,0:T(8,128)(2,1)S(1)} %collective-permute-done.12.refs_17_), channel_id=1, source_target_pairs={{0,4},{2,6},{4,0},{6,2},{8,12},{10,14},{12,8},{14,10},{16,20},{18,... | collective-permute-start | bytes 774152 | tf_op jit(solution)/shard_map/ppermute | solution.py:382
  32.2 16.0 %collective-permute-start.20 = (bf16[1008,128]{1,0:T(8,128)(2,1)S(1)}, bf16[1008,128]{1,0:T(8,128)(2,1)S(1)}, u32[]{:S(2)}, u32[]{:S(2)}) collective-permute-start(bf16[1008,128]{1,0:T(8,128)(2,1)S(1)} %collective-permute-done.12.refs_17_), channel_id=1, source_target_pairs={{0,8},{2,10},{4,12},{6,14},{8,24},{10,26},{12,28},{14,30},{16,0},{... | collective-permute-start | bytes 774152 | tf_op jit(solution)/shard_map/ppermute | solution.py:382
  33.6 10.9 %collective-permute-start.18 = (bf16[576,128]{1,0:T(8,128)(2,1)S(1)}, bf16[576,128]{1,0:T(8,128)(2,1)S(1)}, u32[]{:S(2)}, u32[]{:S(2)}) collective-permute-start(bf16[576,128]{1,0:T(8,128)(2,1)S(1)} %collective-permute-done.10.refs_16_), channel_id=1, source_target_pairs={{0,8},{2,10},{4,12},{6,14},{8,24},{10,26},{12,28},{14,30},{16,0},{... | collective-permute-start | bytes 442376 | tf_op jit(solution)/shard_map/ppermute | solution.py:382
  37.0 8.7 %collective-permute-start.6 = (bf16[576,128]{1,0:T(8,128)(2,1)S(1)}, bf16[576,128]{1,0:T(8,128)(2,1)S(1)}, u32[]{:S(2)}, u32[]{:S(2)}) collective-permute-start(bf16[576,128]{1,0:T(8,128)(2,1)S(1)} %collective-permute-done.3.refs_4_), channel_id=1, source_target_pairs={{0,2},{2,0},{4,6},{6,4},{8,10},{10,8},{12,14},{14,12},{16,18},{18,... | collective-permute-start | bytes 442376 | tf_op jit(solution)/shard_map/ppermute | solution.py:382
  44.6 10.3 %collective-permute-start.7 = (bf16[1008,128]{1,0:T(8,128)(2,1)S(1)}, bf16[1008,128]{1,0:T(8,128)(2,1)S(1)}, u32[]{:S(2)}, u32[]{:S(2)}) collective-permute-start(bf16[1008,128]{1,0:T(8,128)(2,1)S(1)} %collective-permute-done.5.refs_5_), channel_id=1, source_target_pairs={{0,2},{2,0},{4,6},{6,4},{8,10},{10,8},{12,14},{14,12},{16,18},{18,... | collective-permute-start | bytes 774152 | tf_op jit(solution)/shard_map/ppermute | solution.py:382
  54.9 9.5 %collective-permute-start.27 = (bf16[1008,128]{1,0:T(8,128)(2,1)S(1)}, bf16[1008,128]{1,0:T(8,128)(2,1)}, u32[]{:S(2)}, u32[]{:S(2)}) collective-permute-start(bf16[1008,128]{1,0:T(8,128)(2,1)S(1)} %collective-permute-done.21.refs_21_), channel_id=1, source_target_pairs={{0,8},{2,10},{4,12},{6,14},{8,24},{10,26},{12,28},{14,30},{16,0},{... | collective-permute-start | bytes 774152 | tf_op jit(solution)/shard_map/ppermute | solution.py:382
  56.5 8.5 %collective-permute-start.17 = (bf16[1008,128]{1,0:T(8,128)(2,1)S(1)}, bf16[1008,128]{1,0:T(8,128)(2,1)S(1)}, u32[]{:S(2)}, u32[]{:S(2)}) collective-permute-start(bf16[1008,128]{1,0:T(8,128)(2,1)S(1)} %collective-permute-done.12.refs_17_), channel_id=1, source_target_pairs={{0,2},{2,0},{4,6},{6,4},{8,10},{10,8},{12,14},{14,12},{16,18},{18,... | collective-permute-start | bytes 774152 | tf_op jit(solution)/shard_map/ppermute | solution.py:382
  57.2 7.7 %collective-permute-start.15 = (bf16[1008,128]{1,0:T(8,128)(2,1)S(1)}, bf16[1008,128]{1,0:T(8,128)(2,1)S(1)}, u32[]{:S(2)}, u32[]{:S(2)}) collective-permute-start(bf16[1008,128]{1,0:T(8,128)(2,1)S(1)} %collective-permute-done.13.refs_13_), channel_id=1, source_target_pairs={{0,2},{2,0},{4,6},{6,4},{8,10},{10,8},{12,14},{14,12},{16,18},{18,... | collective-permute-start | bytes 774152 | tf_op jit(solution)/shard_map/ppermute | solution.py:382
  196.8 15.6 %collective-permute-start.69 = (bf16[576,128]{1,0:T(8,128)(2,1)S(1)}, bf16[576,128]{1,0:T(8,128)(2,1)S(1)}, u32[]{:S(2)}, u32[]{:S(2)}) collective-permute-start(bf16[576,128]{1,0:T(8,128)(2,1)S(1)} %get-tuple-element.224), channel_id=1, source_target_pairs={{0,2},{2,0},{4,6},{6,4},{8,10},{10,8},{12,14},{14,12},{16,18},{18,... | collective-permute-start | bytes 442376 | tf_op jit(solution)/shard_map/ppermute | solution.py:382
  200.8 8.3 %collective-permute-start.66 = (bf16[1008,128]{1,0:T(8,128)(2,1)S(1)}, bf16[1008,128]{1,0:T(8,128)(2,1)S(1)}, u32[]{:S(2)}, u32[]{:S(2)}) collective-permute-start(bf16[1008,128]{1,0:T(8,128)(2,1)S(1)} %add_convert_fusion.6), channel_id=1, source_target_pairs={{0,8},{2,10},{4,12},{6,14},{8,24},{10,26},{12,28},{14,30},{16,0},{... | collective-permute-start | bytes 774152 | tf_op jit(solution)/shard_map/ppermute | solution.py:382
  203.6 19.9 %collective-permute-start.71 = (bf16[1008,128]{1,0:T(8,128)(2,1)S(1)}, bf16[1008,128]{1,0:T(8,128)(2,1)S(1)}, u32[]{:S(2)}, u32[]{:S(2)}) collective-permute-start(bf16[1008,128]{1,0:T(8,128)(2,1)S(1)} %get-tuple-element.226), channel_id=1, source_target_pairs={{0,2},{2,0},{4,6},{6,4},{8,10},{10,8},{12,14},{14,12},{16,18},{18,... | collective-permute-start | bytes 774152 | tf_op jit(solution)/shard_map/ppermute | solution.py:382
  204.4 9.5 %collective-permute-start.73 = (bf16[1008,128]{1,0:T(8,128)(2,1)S(1)}, bf16[1008,128]{1,0:T(8,128)(2,1)S(1)}, u32[]{:S(2)}, u32[]{:S(2)}) collective-permute-start(bf16[1008,128]{1,0:T(8,128)(2,1)S(1)} %copy-done.88), channel_id=1, source_target_pairs={{0,2},{2,0},{4,6},{6,4},{8,10},{10,8},{12,14},{14,12},{16,18},{18,... | collective-permute-start | bytes 774152 | tf_op jit(solution)/shard_map/ppermute | solution.py:382
  210.2 11.3 %collective-permute-start.64 = (bf16[1008,128]{1,0:T(8,128)(2,1)S(1)}, bf16[1008,128]{1,0:T(8,128)(2,1)S(1)}, u32[]{:S(2)}, u32[]{:S(2)}) collective-permute-start(bf16[1008,128]{1,0:T(8,128)(2,1)S(1)} %add_convert_fusion.7), channel_id=1, source_target_pairs={{0,8},{2,10},{4,12},{6,14},{8,24},{10,26},{12,28},{14,30},{16,0},{... | collective-permute-start | bytes 774152 | tf_op jit(solution)/shard_map/ppermute | solution.py:382
  212.4 9.7 %collective-permute-start.67 = (bf16[1008,128]{1,0:T(8,128)(2,1)S(1)}, bf16[1008,128]{1,0:T(8,128)(2,1)S(1)}, u32[]{:S(2)}, u32[]{:S(2)}) collective-permute-start(bf16[1008,128]{1,0:T(8,128)(2,1)S(1)} %add_convert_fusion.5), channel_id=1, source_target_pairs={{0,4},{2,6},{4,0},{6,2},{8,12},{10,14},{12,8},{14,10},{16,20},{18,... | collective-permute-start | bytes 774152 | tf_op jit(solution)/shard_map/ppermute | solution.py:382
  221.6 16.3 %collective-permute-start.76 = (bf16[1008,128]{1,0:T(8,128)(2,1)S(1)}, bf16[1008,128]{1,0:T(8,128)(2,1)S(1)}, u32[]{:S(2)}, u32[]{:S(2)}) collective-permute-start(bf16[1008,128]{1,0:T(8,128)(2,1)S(1)} %get-tuple-element.236), channel_id=1, source_target_pairs={{0,2},{2,0},{4,6},{6,4},{8,10},{10,8},{12,14},{14,12},{16,18},{18,... | collective-permute-start | bytes 774152 | tf_op jit(solution)/shard_map/ppermute | solution.py:382
  223.5 12.6 %collective-permute-start.74 = (bf16[1008,128]{1,0:T(8,128)(2,1)S(1)}, bf16[1008,128]{1,0:T(8,128)(2,1)S(1)}, u32[]{:S(2)}, u32[]{:S(2)}) collective-permute-start(bf16[1008,128]{1,0:T(8,128)(2,1)S(1)} %add_convert_fusion.3), channel_id=1, source_target_pairs={{0,4},{2,6},{4,0},{6,2},{8,12},{10,14},{12,8},{14,10},{16,20},{18,... | collective-permute-start | bytes 774152 | tf_op jit(solution)/shard_map/ppermute | solution.py:382
  224.3 12.3 %collective-permute-start.72 = (bf16[1008,128]{1,0:T(8,128)(2,1)S(1)}, bf16[1008,128]{1,0:T(8,128)(2,1)S(1)}, u32[]{:S(2)}, u32[]{:S(2)}) collective-permute-start(bf16[1008,128]{1,0:T(8,128)(2,1)S(1)} %add_convert_fusion.4), channel_id=1, source_target_pairs={{0,8},{2,10},{4,12},{6,14},{8,24},{10,26},{12,28},{14,30},{16,0},{... | collective-permute-start | bytes 774152 | tf_op jit(solution)/shard_map/ppermute | solution.py:382
  224.7 11.3 %collective-permute-start.60 = (bf16[576,128]{1,0:T(8,128)(2,1)S(1)}, bf16[576,128]{1,0:T(8,128)(2,1)S(1)}, u32[]{:S(2)}, u32[]{:S(2)}) collective-permute-start(bf16[576,128]{1,0:T(8,128)(2,1)S(1)} %add_convert_fusion.11), channel_id=1, source_target_pairs={{0,8},{2,10},{4,12},{6,14},{8,24},{10,26},{12,28},{14,30},{16,0},{... | collective-permute-start | bytes 442376 | tf_op jit(solution)/shard_map/ppermute | solution.py:382
  228.8 21.7 %collective-permute-start.52 = (bf16[576,128]{1,0:T(8,128)(2,1)S(1)}, bf16[576,128]{1,0:T(8,128)(2,1)S(1)}, u32[]{:S(2)}, u32[]{:S(2)}) collective-permute-start(bf16[576,128]{1,0:T(8,128)(2,1)S(1)} %get-tuple-element.201), channel_id=1, source_target_pairs={{0,2},{2,0},{4,6},{6,4},{8,10},{10,8},{12,14},{14,12},{16,18},{18,... | collective-permute-start | bytes 442376 | tf_op jit(solution)/shard_map/ppermute | solution.py:382
  236.0 14.5 %collective-permute-start.75 = (bf16[1008,128]{1,0:T(8,128)(2,1)S(1)}, bf16[1008,128]{1,0:T(8,128)(2,1)S(1)}, u32[]{:S(2)}, u32[]{:S(2)}) collective-permute-start(bf16[1008,128]{1,0:T(8,128)(2,1)S(1)} %get-tuple-element.234), channel_id=1, source_target_pairs={{0,2},{2,0},{4,6},{6,4},{8,10},{10,8},{12,14},{14,12},{16,18},{18,... | collective-permute-start | bytes 774152 | tf_op jit(solution)/shard_map/ppermute | solution.py:382
  237.9 12.6 %collective-permute-start.79 = (bf16[1008,128]{1,0:T(8,128)(2,1)S(1)}, bf16[1008,128]{1,0:T(8,128)(2,1)S(1)}, u32[]{:S(2)}, u32[]{:S(2)}) collective-permute-start(bf16[1008,128]{1,0:T(8,128)(2,1)S(1)} %add_convert_fusion.1), channel_id=1, source_target_pairs={{0,4},{2,6},{4,0},{6,2},{8,12},{10,14},{12,8},{14,10},{16,20},{18,... | collective-permute-start | bytes 774152 | tf_op jit(solution)/shard_map/ppermute | solution.py:382
  238.7 11.8 %collective-permute-start.77 = (bf16[1008,128]{1,0:T(8,128)(2,1)S(1)}, bf16[1008,128]{1,0:T(8,128)(2,1)S(1)}, u32[]{:S(2)}, u32[]{:S(2)}) collective-permute-start(bf16[1008,128]{1,0:T(8,128)(2,1)S(1)} %add_convert_fusion.2), channel_id=1, source_target_pairs={{0,8},{2,10},{4,12},{6,14},{8,24},{10,26},{12,28},{14,30},{16,0},{... | collective-permute-start | bytes 774152 | tf_op jit(solution)/shard_map/ppermute | solution.py:382
  (137 other events, 671.4 us)

commit v2 on v1

--- a/solution.py
+++ b/solution.py
@@ -83,7 +83,7 @@
         rows_scr[pl.ds(pl.multiple_of(at * 8, 8), 8), :] = part.reshape(8, LANES)
         return carry
 
-    lax.fori_loop(0, whole, load, 0, unroll=4)
+    lax.fori_loop(0, whole, load, 0, unroll=12)
     rows_scr[whole * 8 :, :] = jnp.zeros((rows_in - whole * 8, LANES), F32)
     for at, cols, lanes in split_flat(plan.shard):
         if at >= whole * 8:
@@ -154,7 +154,7 @@
         update(grad, (0, slice(None), cols), main_in, main_out)
         return carry
 
-    lax.fori_loop(0, whole, step, 0, unroll=4)
+    lax.fori_loop(0, whole, step, 0, unroll=24)
     for at, cols, lanes in split_flat(plan.shard):
         if at >= whole * 8:
             update(rows_scr[at : at + 1, 0:lanes], (0, slice(None), cols), main_in, main_out)
@@ -190,7 +190,7 @@
 
 def chunked(total):
     step = total
-    while step > 128 and step % 2 == 0:
+    while step > 256 and step % 2 == 0:
         step //= 2
     return step
 
@@ -204,7 +204,7 @@
     start = pl.multiple_of((owner * plan.shard) // TILE * 16 - origin, 16)
     edge = plan.half // 16
     for src, begin, end, base in ((first, 1, edge, 0), (second, edge, full, edge)):
-        step = largest_step(end - begin, 25)
+        step = largest_step(end - begin, 35)
 
         def move(k, carry, src=src, begin=begin, base=base, step=step):
             to = pl.multiple_of(start + begin * 16 + k * (step * 16), 16)
@@ -345,7 +345,7 @@
         owner = idx_ref[at]
         start = pl.multiple_of((owner * plan.shard) // TILE * 16, 16)
         for out, begin, end in ((outs[2 * at], 0, half), (outs[2 * at + 1], half, plan.rows)):
-            step = 16 * largest_step((end - begin) // 16, 25)
+            step = 16 * largest_step((end - begin) // 16, 36)
 
             def move(k, carry, out=out, begin=begin, step=step, start=start):
                 to = pl.multiple_of(k * step, 16)

time: 259 us -> 254 us (0.981)
  Pallas kernels: 27.5 us -> 22.3 us
    pallas_call x1, Pallas kernels: 10.3 us -> 6.92 us  [pack(): pl.pallas_call(partial(pack_body, plan), out_shape=halves * plan.count, i...]
where the time goes in v2:
time: 254 us; the launch traced here: 253 us
  waiting for transfers between devices  89.3 us (35%)
  starting transfers between devices  69.2 us (27%)
  local copies, waits for them, and re-layouts  31.9 us (13%)
  matrix products  25.1 us (10%)
  Pallas kernels  22.3 us (9%)
  other arithmetic  12.7 us (5%)
  between operations  2.9 us (1%)
    ppermute x80, waiting for transfers between devices, permute(): return lax.ppermute(value, axis, [(at, target(at)) for at in range(count)])  89.3 us
    ppermute x80, starting transfers between devices, permute(): return lax.ppermute(value, axis, [(at, target(at)) for at in range(count)])  69.2 us
    unnamed x183, local copies, waits for them, and re-layouts  28 us
    dot_general x8, matrix products, left_transposed_matmul(): lax.dot_general(left, right, (((0,), (0,)), ((), ())), preferred_element_...  10.5 us
    pallas_call x1, Pallas kernels, unpack(): pl.pallas_call(partial(unpack_body, plan, tuple(which), len(blocks), low,...  7.36 us
    pallas_call x1, Pallas kernels, pack(): pl.pallas_call(partial(pack_body, plan), out_shape=halves * plan.count, i...  6.92 us
    pallas_call x1, Pallas kernels, finish(): pl.pallas_call(partial(finish_body, plan, len(blocks)), out_shape=[flat]...  5.49 us
  transfers between devices with their start and end apart: 80, of which 32 were waited for; matrix products, arithmetic and copies ran while one was open for 5% of the time, Pallas kernels for 0%

profile of v2, /device:TPU:0, one launch (start us, length us, event | category | flops | bytes accessed | tf_op | source)
XLA Modules:
  0.0 253.2 jit_solution(12905540474918757883)
XLA Ops:
  1.3 2.5 shift_out.1
  3.8 3.0 %collective-permute-start.3 = (bf16[576,128]{1,0:T(8,128)(2,1)}, bf16[576,128]{1,0:T(8,128)(2,1)S(1)}, u32[]{:S(2)}, u32[]{:S(2)}) collective-permute-start(bf16[576,128]{1,0:T(8,128)(2,1)} %get-tuple-element.130.refs_0_), channel_id=1, source_target_pairs={{0,4},{2,6},{4,0},{6,2},{8,12},{10,14},{12,8},{14,10},{16,20},{18,... | collective-permute-start | bytes 442376 | tf_op jit(solution)/shard_map/ppermute | solution.py:382
  8.9 2.6 %collective-permute-start.4 = (bf16[1008,128]{1,0:T(8,128)(2,1)}, bf16[1008,128]{1,0:T(8,128)(2,1)S(1)}, u32[]{:S(2)}, u32[]{:S(2)}) collective-permute-start(bf16[1008,128]{1,0:T(8,128)(2,1)} %get-tuple-element.131.refs_1_), channel_id=1, source_target_pairs={{0,8},{2,10},{4,12},{6,14},{8,24},{10,26},{12,28},{14,30},{16,0},{... | collective-permute-start | bytes 774152 | tf_op jit(solution)/shard_map/ppermute | solution.py:382
  12.6 2.0 collective-permute-done.2.refs_8_
  16.4 2.3 collective-permute-done.4.refs_9_
  21.7 3.3 %collective-permute-start.10 = (bf16[576,128]{1,0:T(8,128)(2,1)S(1)}, bf16[576,128]{1,0:T(8,128)(2,1)S(1)}, u32[]{:S(2)}, u32[]{:S(2)}) collective-permute-start(bf16[576,128]{1,0:T(8,128)(2,1)S(1)} %collective-permute-done.2.refs_8_), channel_id=1, source_target_pairs={{0,8},{2,10},{4,12},{6,14},{8,24},{10,26},{12,28},{14,30},{16,0},{... | collective-permute-start | bytes 442376 | tf_op jit(solution)/shard_map/ppermute | solution.py:382
  24.9 3.8 %collective-permute-done.11.refs_12_ = bf16[576,128]{1,0:T(8,128)(2,1)S(1)} collective-permute-done((bf16[576,128]{1,0:T(8,128)(2,1)S(1)}, bf16[576,128]{1,0:T(8,128)(2,1)S(1)}, u32[]{:S(2)}, u32[]{:S(2)}) %collective-permute-start.11) | collective-permute-done | bytes 147488 | tf_op jit(solution)/shard_map/ppermute | solution.py:382
  33.4 3.4 %collective-permute-start.18 = (bf16[576,128]{1,0:T(8,128)(2,1)S(1)}, bf16[576,128]{1,0:T(8,128)(2,1)S(1)}, u32[]{:S(2)}, u32[]{:S(2)}) collective-permute-start(bf16[576,128]{1,0:T(8,128)(2,1)S(1)} %collective-permute-done.10.refs_16_), channel_id=1, source_target_pairs={{0,8},{2,10},{4,12},{6,14},{8,24},{10,26},{12,28},{14,30},{16,0},{... | collective-permute-start | bytes 442376 | tf_op jit(solution)/shard_map/ppermute | solution.py:382
  37.5 6.9 %collective-permute-done.18.refs_24_ = bf16[576,128]{1,0:T(8,128)(2,1)S(1)} collective-permute-done((bf16[576,128]{1,0:T(8,128)(2,1)S(1)}, bf16[576,128]{1,0:T(8,128)(2,1)S(1)}, u32[]{:S(2)}, u32[]{:S(2)}) %collective-permute-start.18) | collective-permute-done | bytes 147488 | tf_op jit(solution)/shard_map/ppermute | solution.py:382
  59.4 4.8 %collective-permute-done.27.refs_29_ = bf16[1008,128]{1,0:T(8,128)(2,1)} collective-permute-done((bf16[1008,128]{1,0:T(8,128)(2,1)S(1)}, bf16[1008,128]{1,0:T(8,128)(2,1)}, u32[]{:S(2)}, u32[]{:S(2)}) %collective-permute-start.27) | collective-permute-done | bytes 258080 | tf_op jit(solution)/shard_map/ppermute | solution.py:382
  79.7 7.4 %shard_map.168 = (bf16[512,1024]{1,0:T(8,128)(2,1)}, f32[1,1024]{1,0:T(1,128)S(1)}, bf16[1024,512]{1,0:T(8,128)(2,1)}, bf16[512,768]{1,0:T(8,128)(2,1)}, bf16[51...) custom-call(s32[16]{0:T(128)S(1)} %stack.120.idx_ref, ...), custom_call_target="tpu_custom_call" | custom-call | bytes 50561024 | tf_op jit(solution)/shard_map/pallas_call | solution.py:289
  92.0 3.6 %collective-permute-done.30 = bf16[128,512]{1,0:T(8,128)(2,1)S(1)} collective-permute-done((bf16[128,512]{1,0:T(8,128)(2,1)S(1)}, bf16[128,512]{1,0:T(8,128)(2,1)S(1)}, u32[]{:S(2)}, u32[]{:S(2)}) %collective-permute-start.30) | collective-permute-done | bytes 131104 | tf_op jit(solution)/shard_map/ppermute | solution.py:382
  103.2 2.0 collective-permute-done.31
  111.5 3.6 %collective-permute-start.37 = (f32[3,256]{1,0:T(4,128)S(1)}, f32[3,256]{1,0:T(4,128)S(1)}, u32[]{:S(2)}, u32[]{:S(2)}) collective-permute-start(f32[3,256]{1,0:T(4,128)S(1)} %add_add_fusion.12), channel_id=1, source_target_pairs={{0,24},{2,26},{4,28},{6,30},{8,16},{10,18},{12,20},{14,22},{16,8},... | collective-permute-start | bytes 9224 | tf_op jit(solution)/shard_map/ppermute | solution.py:382
  116.9 2.7 %collective-permute-done.36 = f32[3,256]{1,0:T(4,128)S(1)} collective-permute-done((f32[3,256]{1,0:T(4,128)S(1)}, f32[3,256]{1,0:T(4,128)S(1)}, u32[]{:S(2)}, u32[]{:S(2)}) %collective-permute-start.36) | collective-permute-done | bytes 3104 | tf_op jit(solution)/shard_map/ppermute | solution.py:382
  121.5 3.4 %collective-permute-done.38 = bf16[128,512]{1,0:T(8,128)(2,1)S(1)} collective-permute-done((bf16[128,512]{1,0:T(8,128)(2,1)S(1)}, bf16[128,512]{1,0:T(8,128)(2,1)S(1)}, u32[]{:S(2)}, u32[]{:S(2)}) %collective-permute-start.38) | collective-permute-done | bytes 131104 | tf_op jit(solution)/shard_map/ppermute | solution.py:382
  128.3 3.4 %collective-permute-done.39 = bf16[128,512]{1,0:T(8,128)(2,1)S(1)} collective-permute-done((bf16[128,512]{1,0:T(8,128)(2,1)S(1)}, bf16[128,512]{1,0:T(8,128)(2,1)S(1)}, u32[]{:S(2)}, u32[]{:S(2)}) %collective-permute-start.39) | collective-permute-done | bytes 131104 | tf_op jit(solution)/shard_map/ppermute | solution.py:382
  147.6 2.3 collective-permute-start.44
  151.6 2.9 %fusion.48 = f32[31,1,256]{2,1,0:T(1,128)S(1)} fusion(f32[1,128,256]{2,1,0:T(8,128)S(1)} %get-tuple-element.278, f32[1,128,256]{2,1,0:T(8,128)S(1)} %multiply_multiply_fusion.1), kind=kOutput, calls=%fused_computation.164 | convolution fusion | flops 11452416 | bytes 293888 | tf_op jit(solution)/shard_map/transpose(jvp())/conv_general_dilated | solution.py:608
  158.4 2.2 collective-permute-done.47
  170.3 2.5 collective-permute-done.48
  181.5 6.9 %pack.1 = (bf16[576,128]{1,0:T(8,128)(2,1)S(1)}, bf16[1008,128]{1,0:T(8,128)(2,1)S(1)}, bf16[576,128]{1,0:T(8,128)(2,1)S(1)}, bf16[1008,128]{1,0:T(8,128)(2,1)S(...) custom-call(s32[16]{0:T(128)S(1)} %stack.120.idx_ref, ...), custom_call_target="tpu_custom_call" | custom-call | tf_op jit(solution)/shard_map/pack/pallas_call | solution.py:367
  192.8 3.5 %collective-permute-done.56 = bf16[576,128]{1,0:T(8,128)(2,1)S(1)} collective-permute-done((bf16[576,128]{1,0:T(8,128)(2,1)S(1)}, bf16[576,128]{1,0:T(8,128)(2,1)S(1)}, u32[]{:S(2)}, u32[]{:S(2)}) %collective-permute-start.56) | collective-permute-done | bytes 147488 | tf_op jit(solution)/shard_map/ppermute | solution.py:382
  196.3 2.0 collective-permute-start.66
  200.0 4.5 %collective-permute-done.66 = bf16[1008,128]{1,0:T(8,128)(2,1)S(1)} collective-permute-done((bf16[1008,128]{1,0:T(8,128)(2,1)S(1)}, bf16[1008,128]{1,0:T(8,128)(2,1)S(1)}, u32[]{:S(2)}, u32[]{:S(2)}) %collective-permute-start.66) | collective-permute-done | bytes 258080 | tf_op jit(solution)/shard_map/ppermute | solution.py:382
  210.1 2.1 collective-permute-done.57
  212.2 4.8 %collective-permute-done.59 = bf16[576,128]{1,0:T(8,128)(2,1)S(1)} collective-permute-done((bf16[576,128]{1,0:T(8,128)(2,1)S(1)}, bf16[576,128]{1,0:T(8,128)(2,1)S(1)}, u32[]{:S(2)}, u32[]{:S(2)}) %collective-permute-start.59) | collective-permute-done | bytes 147488 | tf_op jit(solution)/shard_map/ppermute | solution.py:382
  221.9 2.4 collective-permute-done.62
  224.3 7.2 %collective-permute-done.60 = bf16[576,128]{1,0:T(8,128)(2,1)S(1)} collective-permute-done((bf16[576,128]{1,0:T(8,128)(2,1)S(1)}, bf16[576,128]{1,0:T(8,128)(2,1)S(1)}, u32[]{:S(2)}, u32[]{:S(2)}) %collective-permute-start.60) | collective-permute-done | bytes 147488 | tf_op jit(solution)/shard_map/ppermute | solution.py:382
  234.3 4.4 %collective-permute-done.70.refs_2_ = bf16[576,128]{1,0:T(8,128)(2,1)S(1)} collective-permute-done((bf16[576,128]{1,0:T(8,128)(2,1)S(1)}, bf16[576,128]{1,0:T(8,128)(2,1)S(1)}, u32[]{:S(2)}, u32[]{:S(2)}) %collective-permute-start.70) | collective-permute-done | bytes 147488 | tf_op jit(solution)/shard_map/ppermute | solution.py:382
  239.6 6.3 %collective-permute-done.68.refs_3_ = bf16[576,128]{1,0:T(8,128)(2,1)S(1)} collective-permute-done((bf16[576,128]{1,0:T(8,128)(2,1)S(1)}, bf16[576,128]{1,0:T(8,128)(2,1)S(1)}, u32[]{:S(2)}, u32[]{:S(2)}) %collective-permute-start.68) | collective-permute-done | bytes 147488 | tf_op jit(solution)/shard_map/ppermute | solution.py:382
  247.5 5.5 %finish.1 = (f32[1,1,197344]{2,1,0:T(1,128)}, f32[1,1,197344]{2,1,0:T(1,128)}, f32[1,1,197344]{2,1,0:T(1,128)}, f32[1,1,197344]{2,1,0:T(1,128)}, f32[1,448]{1,0:...) custom-call(s32[3]{0:T(128)} %pad_add_fusion.1.where_ref, bf16[576,128]{1,0:T(8,128)(2,1)} %copy-done.33, ...), custom_call_target="tpu_custom_call" | custom-call | tf_op jit(solution)/shard_map/finish/pallas_call | solution.py:178
  (461 shorter events, 130.0 us)
Async XLA Ops:
  3.8 8.8 %collective-permute-start.3 = (bf16[576,128]{1,0:T(8,128)(2,1)}, bf16[576,128]{1,0:T(8,128)(2,1)S(1)}, u32[]{:S(2)}, u32[]{:S(2)}) collective-permute-start(bf16[576,128]{1,0:T(8,128)(2,1)} %get-tuple-element.130.refs_0_), channel_id=1, source_target_pairs={{0,4},{2,6},{4,0},{6,2},{8,12},{10,14},{12,8},{14,10},{16,20},{18,... | collective-permute-start | bytes 442376 | tf_op jit(solution)/shard_map/ppermute | solution.py:382
  6.8 7.8 %collective-permute-start.2 = (bf16[576,128]{1,0:T(8,128)(2,1)}, bf16[576,128]{1,0:T(8,128)(2,1)S(1)}, u32[]{:S(2)}, u32[]{:S(2)}) collective-permute-start(bf16[576,128]{1,0:T(8,128)(2,1)} %get-tuple-element.130.refs_0_), channel_id=1, source_target_pairs={{0,8},{2,10},{4,12},{6,14},{8,24},{10,26},{12,28},{14,30},{16,0},{... | collective-permute-start | bytes 442376 | tf_op jit(solution)/shard_map/ppermute | solution.py:382
  8.4 8.0 %collective-permute-start.5 = (bf16[1008,128]{1,0:T(8,128)(2,1)}, bf16[1008,128]{1,0:T(8,128)(2,1)S(1)}, u32[]{:S(2)}, u32[]{:S(2)}) collective-permute-start(bf16[1008,128]{1,0:T(8,128)(2,1)} %get-tuple-element.131.refs_1_), channel_id=1, source_target_pairs={{0,4},{2,6},{4,0},{6,2},{8,12},{10,14},{12,8},{14,10},{16,20},{18,... | collective-permute-start | bytes 774152 | tf_op jit(solution)/shard_map/ppermute | solution.py:382
  8.9 9.9 %collective-permute-start.4 = (bf16[1008,128]{1,0:T(8,128)(2,1)}, bf16[1008,128]{1,0:T(8,128)(2,1)S(1)}, u32[]{:S(2)}, u32[]{:S(2)}) collective-permute-start(bf16[1008,128]{1,0:T(8,128)(2,1)} %get-tuple-element.131.refs_1_), channel_id=1, source_target_pairs={{0,8},{2,10},{4,12},{6,14},{8,24},{10,26},{12,28},{14,30},{16,0},{... | collective-permute-start | bytes 774152 | tf_op jit(solution)/shard_map/ppermute | solution.py:382
  18.8 12.7 %collective-permute-start.13 = (bf16[1008,128]{1,0:T(8,128)(2,1)S(1)}, bf16[1008,128]{1,0:T(8,128)(2,1)S(1)}, u32[]{:S(2)}, u32[]{:S(2)}) collective-permute-start(bf16[1008,128]{1,0:T(8,128)(2,1)S(1)} %collective-permute-done.4.refs_9_), channel_id=1, source_target_pairs={{0,4},{2,6},{4,0},{6,2},{8,12},{10,14},{12,8},{14,10},{16,20},{18,... | collective-permute-start | bytes 774152 | tf_op jit(solution)/shard_map/ppermute | solution.py:382
  19.3 12.2 %collective-permute-start.12 = (bf16[1008,128]{1,0:T(8,128)(2,1)S(1)}, bf16[1008,128]{1,0:T(8,128)(2,1)S(1)}, u32[]{:S(2)}, u32[]{:S(2)}) collective-permute-start(bf16[1008,128]{1,0:T(8,128)(2,1)S(1)} %collective-permute-done.4.refs_9_), channel_id=1, source_target_pairs={{0,8},{2,10},{4,12},{6,14},{8,24},{10,26},{12,28},{14,30},{16,0},{... | collective-permute-start | bytes 774152 | tf_op jit(solution)/shard_map/ppermute | solution.py:382
  20.3 8.4 %collective-permute-start.11 = (bf16[576,128]{1,0:T(8,128)(2,1)S(1)}, bf16[576,128]{1,0:T(8,128)(2,1)S(1)}, u32[]{:S(2)}, u32[]{:S(2)}) collective-permute-start(bf16[576,128]{1,0:T(8,128)(2,1)S(1)} %collective-permute-done.2.refs_8_), channel_id=1, source_target_pairs={{0,4},{2,6},{4,0},{6,2},{8,12},{10,14},{12,8},{14,10},{16,20},{18,... | collective-permute-start | bytes 442376 | tf_op jit(solution)/shard_map/ppermute | solution.py:382
  21.7 8.3 %collective-permute-start.10 = (bf16[576,128]{1,0:T(8,128)(2,1)S(1)}, bf16[576,128]{1,0:T(8,128)(2,1)S(1)}, u32[]{:S(2)}, u32[]{:S(2)}) collective-permute-start(bf16[576,128]{1,0:T(8,128)(2,1)S(1)} %collective-permute-done.2.refs_8_), channel_id=1, source_target_pairs={{0,8},{2,10},{4,12},{6,14},{8,24},{10,26},{12,28},{14,30},{16,0},{... | collective-permute-start | bytes 442376 | tf_op jit(solution)/shard_map/ppermute | solution.py:382
  24.9 7.8 %collective-permute-start = (bf16[576,128]{1,0:T(8,128)(2,1)}, bf16[576,128]{1,0:T(8,128)(2,1)S(1)}, u32[]{:S(2)}, u32[]{:S(2)}) collective-permute-start(bf16[576,128]{1,0:T(8,128)(2,1)} %get-tuple-element.130.refs_0_), channel_id=1, source_target_pairs={{0,2},{2,0},{4,6},{6,4},{8,10},{10,8},{12,14},{14,12},{16,18},{18,... | collective-permute-start | bytes 442376 | tf_op jit(solution)/shard_map/ppermute | solution.py:382
  31.4 13.0 %collective-permute-start.1 = (bf16[1008,128]{1,0:T(8,128)(2,1)}, bf16[1008,128]{1,0:T(8,128)(2,1)S(1)}, u32[]{:S(2)}, u32[]{:S(2)}) collective-permute-start(bf16[1008,128]{1,0:T(8,128)(2,1)} %get-tuple-element.131.refs_1_), channel_id=1, source_target_pairs={{0,2},{2,0},{4,6},{6,4},{8,10},{10,8},{12,14},{14,12},{16,18},{18,... | collective-permute-start | bytes 774152 | tf_op jit(solution)/shard_map/ppermute | solution.py:382
  31.4 15.5 %collective-permute-start.21 = (bf16[1008,128]{1,0:T(8,128)(2,1)S(1)}, bf16[1008,128]{1,0:T(8,128)(2,1)S(1)}, u32[]{:S(2)}, u32[]{:S(2)}) collective-permute-start(bf16[1008,128]{1,0:T(8,128)(2,1)S(1)} %collective-permute-done.12.refs_17_), channel_id=1, source_target_pairs={{0,4},{2,6},{4,0},{6,2},{8,12},{10,14},{12,8},{14,10},{16,20},{18,... | collective-permute-start | bytes 774152 | tf_op jit(solution)/shard_map/ppermute | solution.py:382
  32.0 16.0 %collective-permute-start.20 = (bf16[1008,128]{1,0:T(8,128)(2,1)S(1)}, bf16[1008,128]{1,0:T(8,128)(2,1)S(1)}, u32[]{:S(2)}, u32[]{:S(2)}) collective-permute-start(bf16[1008,128]{1,0:T(8,128)(2,1)S(1)} %collective-permute-done.12.refs_17_), channel_id=1, source_target_pairs={{0,8},{2,10},{4,12},{6,14},{8,24},{10,26},{12,28},{14,30},{16,0},{... | collective-permute-start | bytes 774152 | tf_op jit(solution)/shard_map/ppermute | solution.py:382
  33.4 10.9 %collective-permute-start.18 = (bf16[576,128]{1,0:T(8,128)(2,1)S(1)}, bf16[576,128]{1,0:T(8,128)(2,1)S(1)}, u32[]{:S(2)}, u32[]{:S(2)}) collective-permute-start(bf16[576,128]{1,0:T(8,128)(2,1)S(1)} %collective-permute-done.10.refs_16_), channel_id=1, source_target_pairs={{0,8},{2,10},{4,12},{6,14},{8,24},{10,26},{12,28},{14,30},{16,0},{... | collective-permute-start | bytes 442376 | tf_op jit(solution)/shard_map/ppermute | solution.py:382
  36.8 8.7 %collective-permute-start.6 = (bf16[576,128]{1,0:T(8,128)(2,1)S(1)}, bf16[576,128]{1,0:T(8,128)(2,1)S(1)}, u32[]{:S(2)}, u32[]{:S(2)}) collective-permute-start(bf16[576,128]{1,0:T(8,128)(2,1)S(1)} %collective-permute-done.3.refs_4_), channel_id=1, source_target_pairs={{0,2},{2,0},{4,6},{6,4},{8,10},{10,8},{12,14},{14,12},{16,18},{18,... | collective-permute-start | bytes 442376 | tf_op jit(solution)/shard_map/ppermute | solution.py:382
  44.4 10.3 %collective-permute-start.7 = (bf16[1008,128]{1,0:T(8,128)(2,1)S(1)}, bf16[1008,128]{1,0:T(8,128)(2,1)S(1)}, u32[]{:S(2)}, u32[]{:S(2)}) collective-permute-start(bf16[1008,128]{1,0:T(8,128)(2,1)S(1)} %collective-permute-done.5.refs_5_), channel_id=1, source_target_pairs={{0,2},{2,0},{4,6},{6,4},{8,10},{10,8},{12,14},{14,12},{16,18},{18,... | collective-permute-start | bytes 774152 | tf_op jit(solution)/shard_map/ppermute | solution.py:382
  54.7 9.5 %collective-permute-start.27 = (bf16[1008,128]{1,0:T(8,128)(2,1)S(1)}, bf16[1008,128]{1,0:T(8,128)(2,1)}, u32[]{:S(2)}, u32[]{:S(2)}) collective-permute-start(bf16[1008,128]{1,0:T(8,128)(2,1)S(1)} %collective-permute-done.21.refs_21_), channel_id=1, source_target_pairs={{0,8},{2,10},{4,12},{6,14},{8,24},{10,26},{12,28},{14,30},{16,0},{... | collective-permute-start | bytes 774152 | tf_op jit(solution)/shard_map/ppermute | solution.py:382
  56.3 8.5 %collective-permute-start.17 = (bf16[1008,128]{1,0:T(8,128)(2,1)S(1)}, bf16[1008,128]{1,0:T(8,128)(2,1)S(1)}, u32[]{:S(2)}, u32[]{:S(2)}) collective-permute-start(bf16[1008,128]{1,0:T(8,128)(2,1)S(1)} %collective-permute-done.12.refs_17_), channel_id=1, source_target_pairs={{0,2},{2,0},{4,6},{6,4},{8,10},{10,8},{12,14},{14,12},{16,18},{18,... | collective-permute-start | bytes 774152 | tf_op jit(solution)/shard_map/ppermute | solution.py:382
  57.0 7.7 %collective-permute-start.15 = (bf16[1008,128]{1,0:T(8,128)(2,1)S(1)}, bf16[1008,128]{1,0:T(8,128)(2,1)S(1)}, u32[]{:S(2)}, u32[]{:S(2)}) collective-permute-start(bf16[1008,128]{1,0:T(8,128)(2,1)S(1)} %collective-permute-done.13.refs_13_), channel_id=1, source_target_pairs={{0,2},{2,0},{4,6},{6,4},{8,10},{10,8},{12,14},{14,12},{16,18},{18,... | collective-permute-start | bytes 774152 | tf_op jit(solution)/shard_map/ppermute | solution.py:382
  192.2 15.6 %collective-permute-start.69 = (bf16[576,128]{1,0:T(8,128)(2,1)S(1)}, bf16[576,128]{1,0:T(8,128)(2,1)S(1)}, u32[]{:S(2)}, u32[]{:S(2)}) collective-permute-start(bf16[576,128]{1,0:T(8,128)(2,1)S(1)} %get-tuple-element.224), channel_id=1, source_target_pairs={{0,2},{2,0},{4,6},{6,4},{8,10},{10,8},{12,14},{14,12},{16,18},{18,... | collective-permute-start | bytes 442376 | tf_op jit(solution)/shard_map/ppermute | solution.py:382
  196.3 8.3 %collective-permute-start.66 = (bf16[1008,128]{1,0:T(8,128)(2,1)S(1)}, bf16[1008,128]{1,0:T(8,128)(2,1)S(1)}, u32[]{:S(2)}, u32[]{:S(2)}) collective-permute-start(bf16[1008,128]{1,0:T(8,128)(2,1)S(1)} %add_convert_fusion.6), channel_id=1, source_target_pairs={{0,8},{2,10},{4,12},{6,14},{8,24},{10,26},{12,28},{14,30},{16,0},{... | collective-permute-start | bytes 774152 | tf_op jit(solution)/shard_map/ppermute | solution.py:382
  199.0 19.9 %collective-permute-start.71 = (bf16[1008,128]{1,0:T(8,128)(2,1)S(1)}, bf16[1008,128]{1,0:T(8,128)(2,1)S(1)}, u32[]{:S(2)}, u32[]{:S(2)}) collective-permute-start(bf16[1008,128]{1,0:T(8,128)(2,1)S(1)} %get-tuple-element.226), channel_id=1, source_target_pairs={{0,2},{2,0},{4,6},{6,4},{8,10},{10,8},{12,14},{14,12},{16,18},{18,... | collective-permute-start | bytes 774152 | tf_op jit(solution)/shard_map/ppermute | solution.py:382
  199.8 9.5 %collective-permute-start.73 = (bf16[1008,128]{1,0:T(8,128)(2,1)S(1)}, bf16[1008,128]{1,0:T(8,128)(2,1)S(1)}, u32[]{:S(2)}, u32[]{:S(2)}) collective-permute-start(bf16[1008,128]{1,0:T(8,128)(2,1)S(1)} %copy-done.88), channel_id=1, source_target_pairs={{0,2},{2,0},{4,6},{6,4},{8,10},{10,8},{12,14},{14,12},{16,18},{18,... | collective-permute-start | bytes 774152 | tf_op jit(solution)/shard_map/ppermute | solution.py:382
  205.7 11.3 %collective-permute-start.64 = (bf16[1008,128]{1,0:T(8,128)(2,1)S(1)}, bf16[1008,128]{1,0:T(8,128)(2,1)S(1)}, u32[]{:S(2)}, u32[]{:S(2)}) collective-permute-start(bf16[1008,128]{1,0:T(8,128)(2,1)S(1)} %add_convert_fusion.7), channel_id=1, source_target_pairs={{0,8},{2,10},{4,12},{6,14},{8,24},{10,26},{12,28},{14,30},{16,0},{... | collective-permute-start | bytes 774152 | tf_op jit(solution)/shard_map/ppermute | solution.py:382
  207.8 9.7 %collective-permute-start.67 = (bf16[1008,128]{1,0:T(8,128)(2,1)S(1)}, bf16[1008,128]{1,0:T(8,128)(2,1)S(1)}, u32[]{:S(2)}, u32[]{:S(2)}) collective-permute-start(bf16[1008,128]{1,0:T(8,128)(2,1)S(1)} %add_convert_fusion.5), channel_id=1, source_target_pairs={{0,4},{2,6},{4,0},{6,2},{8,12},{10,14},{12,8},{14,10},{16,20},{18,... | collective-permute-start | bytes 774152 | tf_op jit(solution)/shard_map/ppermute | solution.py:382
  217.0 16.3 %collective-permute-start.76 = (bf16[1008,128]{1,0:T(8,128)(2,1)S(1)}, bf16[1008,128]{1,0:T(8,128)(2,1)S(1)}, u32[]{:S(2)}, u32[]{:S(2)}) collective-permute-start(bf16[1008,128]{1,0:T(8,128)(2,1)S(1)} %get-tuple-element.236), channel_id=1, source_target_pairs={{0,2},{2,0},{4,6},{6,4},{8,10},{10,8},{12,14},{14,12},{16,18},{18,... | collective-permute-start | bytes 774152 | tf_op jit(solution)/shard_map/ppermute | solution.py:382
  218.9 12.6 %collective-permute-start.74 = (bf16[1008,128]{1,0:T(8,128)(2,1)S(1)}, bf16[1008,128]{1,0:T(8,128)(2,1)S(1)}, u32[]{:S(2)}, u32[]{:S(2)}) collective-permute-start(bf16[1008,128]{1,0:T(8,128)(2,1)S(1)} %add_convert_fusion.3), channel_id=1, source_target_pairs={{0,4},{2,6},{4,0},{6,2},{8,12},{10,14},{12,8},{14,10},{16,20},{18,... | collective-permute-start | bytes 774152 | tf_op jit(solution)/shard_map/ppermute | solution.py:382
  219.7 12.3 %collective-permute-start.72 = (bf16[1008,128]{1,0:T(8,128)(2,1)S(1)}, bf16[1008,128]{1,0:T(8,128)(2,1)S(1)}, u32[]{:S(2)}, u32[]{:S(2)}) collective-permute-start(bf16[1008,128]{1,0:T(8,128)(2,1)S(1)} %add_convert_fusion.4), channel_id=1, source_target_pairs={{0,8},{2,10},{4,12},{6,14},{8,24},{10,26},{12,28},{14,30},{16,0},{... | collective-permute-start | bytes 774152 | tf_op jit(solution)/shard_map/ppermute | solution.py:382
  220.2 11.3 %collective-permute-start.60 = (bf16[576,128]{1,0:T(8,128)(2,1)S(1)}, bf16[576,128]{1,0:T(8,128)(2,1)S(1)}, u32[]{:S(2)}, u32[]{:S(2)}) collective-permute-start(bf16[576,128]{1,0:T(8,128)(2,1)S(1)} %add_convert_fusion.11), channel_id=1, source_target_pairs={{0,8},{2,10},{4,12},{6,14},{8,24},{10,26},{12,28},{14,30},{16,0},{... | collective-permute-start | bytes 442376 | tf_op jit(solution)/shard_map/ppermute | solution.py:382
  224.3 21.7 %collective-permute-start.52 = (bf16[576,128]{1,0:T(8,128)(2,1)S(1)}, bf16[576,128]{1,0:T(8,128)(2,1)S(1)}, u32[]{:S(2)}, u32[]{:S(2)}) collective-permute-start(bf16[576,128]{1,0:T(8,128)(2,1)S(1)} %get-tuple-element.201), channel_id=1, source_target_pairs={{0,2},{2,0},{4,6},{6,4},{8,10},{10,8},{12,14},{14,12},{16,18},{18,... | collective-permute-start | bytes 442376 | tf_op jit(solution)/shard_map/ppermute | solution.py:382
  231.5 14.5 %collective-permute-start.75 = (bf16[1008,128]{1,0:T(8,128)(2,1)S(1)}, bf16[1008,128]{1,0:T(8,128)(2,1)S(1)}, u32[]{:S(2)}, u32[]{:S(2)}) collective-permute-start(bf16[1008,128]{1,0:T(8,128)(2,1)S(1)} %get-tuple-element.234), channel_id=1, source_target_pairs={{0,2},{2,0},{4,6},{6,4},{8,10},{10,8},{12,14},{14,12},{16,18},{18,... | collective-permute-start | bytes 774152 | tf_op jit(solution)/shard_map/ppermute | solution.py:382
  233.4 12.6 %collective-permute-start.79 = (bf16[1008,128]{1,0:T(8,128)(2,1)S(1)}, bf16[1008,128]{1,0:T(8,128)(2,1)S(1)}, u32[]{:S(2)}, u32[]{:S(2)}) collective-permute-start(bf16[1008,128]{1,0:T(8,128)(2,1)S(1)} %add_convert_fusion.1), channel_id=1, source_target_pairs={{0,4},{2,6},{4,0},{6,2},{8,12},{10,14},{12,8},{14,10},{16,20},{18,... | collective-permute-start | bytes 774152 | tf_op jit(solution)/shard_map/ppermute | solution.py:382
  234.2 11.8 %collective-permute-start.77 = (bf16[1008,128]{1,0:T(8,128)(2,1)S(1)}, bf16[1008,128]{1,0:T(8,128)(2,1)S(1)}, u32[]{:S(2)}, u32[]{:S(2)}) collective-permute-start(bf16[1008,128]{1,0:T(8,128)(2,1)S(1)} %add_convert_fusion.2), channel_id=1, source_target_pairs={{0,8},{2,10},{4,12},{6,14},{8,24},{10,26},{12,28},{14,30},{16,0},{... | collective-permute-start | bytes 774152 | tf_op jit(solution)/shard_map/ppermute | solution.py:382
  (137 other events, 670.3 us)
